TPU v7x, 32 devices: a whole 2x2x4 slice. The times are simulated.
32 devices in a mesh: band: 4 (over x, core), gvec: 2 (over y), dom: 4 (over z).
Axes of the slice: x: 2, y: 2, z: 4, core: 2. Of those that a mesh axis runs over, the one named last changes fastest.
Arguments:
- coeffs: bfloat16 [16, 128, 128, 128], P(('band', 'dom'), 'gvec'), may hold values from -1.5 to 1.5
- v_local: bfloat16 [128, 128, 128], P(None, 'gvec'), may hold values from -4 to 4
- atom_pos: float32 [3, 32768], P(None, ('band', 'gvec', 'dom')), may hold values from -32 to 160
- atom_charge: float32 [32768], P(('band', 'gvec', 'dom')), may hold values from -1 to 1
- near_list: int32 [512], P(('band', 'gvec', 'dom')), may hold values from 0 to 1023, as said below
- live_count: int32 [32], P(('band', 'gvec', 'dom')), may hold values from 0 to 16, as said below
Outputs:
- waves_new: bfloat16 [16, 128, 128, 128], P(('band', 'dom'), 'gvec')
- energies: float32 [16], P(('band', 'dom'))
- resid_ratio: float32 [16], P(('band', 'dom'))
- atom_force: float32 [3, 32768], P(None, ('band', 'gvec', 'dom'))
- totals: float32 [8], replicated
Inputs may be any that keep to these rules, and one draw needn't show every extreme that they name: `live_count`: the counts of all devices sum to exactly 128; some device has all 16 slots live; a device's live slots are its first ones. `near_list`: indices of the device's own atoms; the 16 entries of one device's block are distinct.
All inputs are finite; a program needn't handle non-finite values.
Results may differ from a plain program's by a relative error of at most 0.0045.
Values may be sent and summed in bfloat16 or wider, within the bound.
A program may use at most 64 MiB of HBM per device.

v0:
```python
import jax
import jax.numpy as jnp
from jax import lax
from jax.experimental import pallas as pl
from jax.experimental.pallas import tpu as pltpu
from jax.sharding import PartitionSpec as P
import functools

sigma_fractions = (1.0 / 32.0, 1.0 / 16.0, 1.0 / 8.0, 1.0 / 4.0)
kernel_weights = (1.0, 0.5, 0.25, 0.125)
force_unit = 1.0 / 4096.0
step_size = 0.5


def cosine_table(length):
    points = jnp.arange(length).astype(jnp.float32)
    angles = jnp.pi * (points[:, None] + 0.5) * points[None, :] / length
    scales = jnp.where(points == 0.0, jnp.sqrt(1.0 / length), jnp.sqrt(2.0 / length))
    return (jnp.cos(angles) * scales[None, :]).astype(jnp.bfloat16)


def occupancy(band_index, band_total):
    shifted = band_index.astype(jnp.float32) - 0.5 * band_total
    return 2.0 / (1.0 + jnp.exp(shifted / (0.125 * band_total)))


def kernels(points, centres, extent):
    values = []
    slopes = []
    for fraction in sigma_fractions:
        exponent = 0.5 / (extent * fraction) ** 2
        offset = points[:, None] - centres[None, :]
        gauss_value = jnp.exp(-exponent * offset * offset)
        values.append(gauss_value)
        slopes.append(2.0 * exponent * offset * gauss_value)
    return (jnp.concatenate(values, axis=1), jnp.concatenate(slopes, axis=1))


def peer_coords(index, sizes):
    _, gvec_size, dom_size = sizes
    return (index // (gvec_size * dom_size), (index // dom_size) % gvec_size, index % dom_size)


def gather_kernel(sizes, x_ref, out_ref, send_sem, recv_sem):
    total = sizes[0] * sizes[1] * sizes[2]
    me = (lax.axis_index("band") * sizes[1] + lax.axis_index("gvec")) * sizes[2] + lax.axis_index("dom")
    barrier = pltpu.get_barrier_semaphore()

    def greet(step, carry):
        peer = lax.rem(me + step, total)
        pl.semaphore_signal(
            barrier, inc=1, device_id=peer_coords(peer, sizes), device_id_type=pl.DeviceIdType.MESH
        )
        return carry

    def copy_of(step):
        peer = lax.rem(me + step, total)
        return pltpu.make_async_remote_copy(
            src_ref=x_ref,
            dst_ref=out_ref.at[me],
            send_sem=send_sem.at[step],
            recv_sem=recv_sem.at[step],
            device_id=peer_coords(peer, sizes),
            device_id_type=pl.DeviceIdType.MESH,
        )

    def send(step, carry):
        copy_of(step).start()
        return carry

    def finish(step, carry):
        copy_of(step).wait()
        return carry

    lax.fori_loop(1, total, greet, 0)
    out_ref[me] = x_ref[...]
    pl.semaphore_wait(barrier, total - 1)
    lax.fori_loop(1, total, send, 0)
    lax.fori_loop(1, total, finish, 0)


def gather_all(block, sizes, collective_id):
    total = sizes[0] * sizes[1] * sizes[2]
    return pl.pallas_call(
        functools.partial(gather_kernel, sizes),
        out_shape=jax.ShapeDtypeStruct((total,) + block.shape, block.dtype),
        in_specs=[pl.BlockSpec(memory_space=pltpu.VMEM)],
        out_specs=pl.BlockSpec(memory_space=pltpu.VMEM),
        scratch_shapes=[pltpu.SemaphoreType.DMA((total,)), pltpu.SemaphoreType.DMA((total,))],
        compiler_params=pltpu.CompilerParams(collective_id=collective_id, has_side_effects=True),
        name=f"gather_{collective_id}",
    )(block)


def plane_rows(x_ref, y_ref):
    rows, width = x_ref.shape
    y_total = y_ref.shape[0]
    parts = []
    for row in range(rows):
        parts.append((x_ref[row : row + 1, :] * y_ref[...]).astype(jnp.bfloat16))
    return jnp.concatenate(parts, axis=0)


def potential_kernel(x_ref, y_ref, depth_ref, local_ref, out_ref):
    value = lax.dot_general(
        plane_rows(x_ref, y_ref),
        depth_ref[...],
        (((1,), (1,)), ((), ())),
        preferred_element_type=jnp.float32,
    )
    rounded = value.astype(jnp.bfloat16).astype(jnp.float32).reshape(out_ref.shape)
    out_ref[...] = local_ref[...].astype(jnp.float32) + rounded


def slab_potential(x_value, y_value, depth, v_local):
    x_total, y_total, z_total = v_local.shape
    width = x_value.shape[1]
    rows = 16
    return pl.pallas_call(
        potential_kernel,
        grid=(x_total // rows,),
        out_shape=jax.ShapeDtypeStruct(v_local.shape, jnp.float32),
        in_specs=[
            pl.BlockSpec((rows, width), lambda i: (i, 0)),
            pl.BlockSpec((y_total, width), lambda i: (0, 0)),
            pl.BlockSpec((z_total, width), lambda i: (0, 0)),
            pl.BlockSpec((rows, y_total, z_total), lambda i: (i, 0, 0)),
        ],
        out_specs=pl.BlockSpec((rows, y_total, z_total), lambda i: (i, 0, 0)),
        cost_estimate=pl.CostEstimate(
            flops=8 * x_total * y_total * z_total * width,
            bytes_accessed=6 * x_total * y_total * z_total,
            transcendentals=0,
        ),
        name="slab_potential",
    )(x_value, y_value, depth, v_local)


def force_kernel(xv_ref, xs_ref, yv_ref, ys_ref, real_ref, out_ref):
    @pl.when(pl.program_id(0) == 0)
    def _():
        out_ref[...] = jnp.zeros_like(out_ref)

    rows, y_total, z_total = real_ref.shape
    density = real_ref[...].astype(jnp.float32)
    density = (density * density).astype(jnp.bfloat16).reshape(rows * y_total, z_total)
    for part, (xr, yr) in enumerate(((xv_ref, yv_ref), (xs_ref, yv_ref), (xv_ref, ys_ref))):
        out_ref[part] += lax.dot_general(
            density,
            plane_rows(xr, yr),
            (((0,), (0,)), ((), ())),
            preferred_element_type=jnp.float32,
        )


def slab_moments(x_value, x_slope, y_value, y_slope, real_space):
    x_total, y_total, z_total = real_space.shape
    width = x_value.shape[1]
    rows = 16
    return pl.pallas_call(
        force_kernel,
        grid=(x_total // rows,),
        out_shape=jax.ShapeDtypeStruct((3, z_total, width), jnp.float32),
        in_specs=[
            pl.BlockSpec((rows, width), lambda i: (i, 0)),
            pl.BlockSpec((rows, width), lambda i: (i, 0)),
            pl.BlockSpec((y_total, width), lambda i: (0, 0)),
            pl.BlockSpec((y_total, width), lambda i: (0, 0)),
            pl.BlockSpec((rows, y_total, z_total), lambda i: (i, 0, 0)),
        ],
        out_specs=pl.BlockSpec((3, z_total, width), lambda i: (0, 0, 0)),
        cost_estimate=pl.CostEstimate(
            flops=12 * x_total * y_total * z_total * width,
            bytes_accessed=2 * x_total * y_total * z_total,
            transcendentals=0,
        ),
        name="slab_moments",
    )(x_value, x_slope, y_value, y_slope, real_space)


def tail_kernel(
    sizes, base, back_ref, coeff_ref, table_ref, weight_ref, head_ref,
    waves_ref, out_ref, image_ref, sums_ref, tile_ref, send_sem, recv_sem,
):
    band_size, gvec_size, dom_size = sizes
    total = band_size * gvec_size * dom_size
    band_id, gvec_id, dom_id = lax.axis_index("band"), lax.axis_index("gvec"), lax.axis_index("dom")
    me = (band_id * gvec_size + gvec_id) * dom_size + dom_id
    local_bands, x_local, extent, _ = coeff_ref.shape
    barrier = pltpu.get_barrier_semaphore()

    def peer_of(step):
        outer = step // gvec_size
        return (
            lax.rem(band_id + outer // dom_size, band_size),
            lax.rem(gvec_id + step % gvec_size, gvec_size),
            lax.rem(dom_id + outer % dom_size, dom_size),
        )

    def greet(step, carry):
        pl.semaphore_signal(
            barrier, inc=1, device_id=peer_of(step), device_id_type=pl.DeviceIdType.MESH
        )
        return carry

    lax.fori_loop(1, total, greet, 0)

    def copy_of(step):
        return pltpu.make_async_remote_copy(
            src_ref=tile_ref,
            dst_ref=out_ref.at[me],
            send_sem=send_sem.at[step],
            recv_sem=recv_sem.at[step],
            device_id=peer_of(step),
            device_id_type=pl.DeviceIdType.MESH,
        )

    def send(step, carry):
        copy_of(step).start()
        return carry

    def finish(step, carry):
        copy_of(step).wait()
        return carry

    rows = 4
    block = (rows, extent, extent)
    wave_step = jnp.pi / extent
    q_wave = lax.broadcasted_iota(jnp.int32, block[1:], 0).astype(jnp.float32) * wave_step
    l_wave = lax.broadcasted_iota(jnp.int32, block[1:], 1).astype(jnp.float32) * wave_step
    plane_kinetic = 0.5 * (q_wave * q_wave + l_wave * l_wave)

    def x_waves(index):
        first = gvec_id * x_local + index * rows
        at = lax.broadcasted_iota(jnp.int32, block, 0) + first
        return at.astype(jnp.float32) * wave_step

    def total_of(value):
        return jnp.sum(jnp.sum(value, axis=0, keepdims=True), axis=1, keepdims=True)

    spots = (
        lax.broadcasted_iota(jnp.int32, head_ref.shape, 0) * 128
        + lax.broadcasted_iota(jnp.int32, head_ref.shape, 1)
    )
    tile = head_ref[...]
    stress = [0.0] * 6
    for band in range(local_bands):
        sums_ref[...] = jnp.zeros_like(sums_ref)

        def first_pass(index, carry):
            window = pl.ds(index * rows, rows)
            wide = coeff_ref[band, window].astype(jnp.float32)
            field = jnp.dot(
                back_ref[band, window].reshape(rows * extent, extent),
                table_ref[...],
                preferred_element_type=jnp.float32,
            ).reshape(block)
            x_wave = x_waves(index)
            image = (0.5 * x_wave * x_wave + plane_kinetic[None]) * wide + field
            image_ref[band, window] = image
            square = wide * wide
            by_x = square * x_wave
            sums_ref[0] += jnp.sum(square, axis=0)
            sums_ref[1] += jnp.sum(by_x, axis=0)
            sums_ref[2] += jnp.sum(by_x * x_wave, axis=0)
            sums_ref[3] += jnp.sum(wide * image, axis=0)
            return carry

        lax.fori_loop(0, x_local // rows, first_pass, 0)
        norm = total_of(sums_ref[0])
        inner = total_of(sums_ref[3])
        filled = norm > 0.0
        energy = jnp.where(filled, inner / jnp.where(filled, norm, 1.0), 0.0)
        weight = weight_ref[0:1, band : band + 1]
        terms = (
            sums_ref[2],
            sums_ref[0] * q_wave * q_wave,
            sums_ref[0] * l_wave * l_wave,
            sums_ref[1] * q_wave,
            sums_ref[1] * l_wave,
            sums_ref[0] * q_wave * l_wave,
        )
        stress = [old + weight * total_of(term) for old, term in zip(stress, terms)]
        sums_ref[1] = jnp.zeros_like(sums_ref[1])

        def second_pass(index, carry):
            window = pl.ds(index * rows, rows)
            wide = coeff_ref[band, window].astype(jnp.float32)
            residual = image_ref[band, window] - energy[None] * wide
            sums_ref[1] += jnp.sum(residual * residual, axis=0)
            return carry

        lax.fori_loop(0, x_local // rows, second_pass, 0)
        square = total_of(sums_ref[1])
        for shift, value in enumerate((norm, inner, square)):
            tile = jnp.where(spots == base + 7 + shift * local_bands + band, value, tile)
    for shift, value in enumerate(stress):
        tile = jnp.where(spots == base + shift, value / float(extent**3), tile)
    tile_ref[...] = tile
    out_ref[me] = tile
    pl.semaphore_wait(barrier, total - 1)
    lax.fori_loop(1, total, send, 0)
    lax.fori_loop(1, gvec_size, finish, 0)

    both = tile
    for step in range(1, gvec_size):
        other = lax.rem(gvec_id + step, gvec_size)
        both = both + out_ref[(band_id * gvec_size + other) * dom_size + dom_id]
    for band in range(local_bands):
        norm = total_of(jnp.where(spots == base + 7 + band, both, 0.0))
        inner = total_of(jnp.where(spots == base + 7 + local_bands + band, both, 0.0))
        energy = inner / norm

        def last_pass(index, carry):
            window = pl.ds(index * rows, rows)
            wide = coeff_ref[band, window].astype(jnp.float32)
            x_wave = x_waves(index)
            kinetic = 0.5 * x_wave * x_wave + plane_kinetic[None]
            residual = image_ref[band, window] - energy[None] * wide
            updated = wide - step_size * residual / (1.0 + kinetic)
            waves_ref[band, window] = updated.astype(jnp.bfloat16)
            return carry

        lax.fori_loop(0, x_local // rows, last_pass, 0)
    lax.fori_loop(gvec_size, total, finish, 0)


def tail(back_two, coeffs, cosines, weight, head, base, sizes):
    total = sizes[0] * sizes[1] * sizes[2]
    extent = coeffs.shape[-1]
    vmem = pl.BlockSpec(memory_space=pltpu.VMEM)
    return pl.pallas_call(
        functools.partial(tail_kernel, sizes, base),
        out_shape=(
            jax.ShapeDtypeStruct(coeffs.shape, jnp.bfloat16),
            jax.ShapeDtypeStruct((total,) + head.shape, jnp.float32),
        ),
        in_specs=[vmem] * 5,
        out_specs=(vmem, vmem),
        scratch_shapes=[
            pltpu.VMEM(coeffs.shape, jnp.float32),
            pltpu.VMEM((4, extent, extent), jnp.float32),
            pltpu.VMEM(head.shape, jnp.float32),
            pltpu.SemaphoreType.DMA((total,)),
            pltpu.SemaphoreType.DMA((total,)),
        ],
        compiler_params=pltpu.CompilerParams(
            collective_id=1, has_side_effects=True, vmem_limit_bytes=40 * 1024 * 1024
        ),
        name="tail",
    )(back_two, coeffs, cosines, weight, head)


def per_device(sizes, coeffs, v_local, atom_pos, atom_charge, near_list, live_count):
    local_bands, x_local, extent, _ = coeffs.shape
    cosines = cosine_table(extent)
    gvec_id = lax.axis_index("gvec")
    group_id = lax.axis_index("band") * sizes[2] + lax.axis_index("dom")
    me = (lax.axis_index("band") * sizes[1] + gvec_id) * sizes[2] + lax.axis_index("dom")
    groups = sizes[0] * sizes[2]
    devices = groups * sizes[1]
    band_total = local_bands * groups
    cell_count = float(extent**3)
    band_ids = group_id * local_bands + jnp.arange(local_bands)
    weight = occupancy(band_ids, band_total)
    capacity = near_list.shape[0]
    live_mask = (jnp.arange(capacity) < live_count[0]).astype(jnp.float32)
    picked_pos = jnp.take(atom_pos, near_list, axis=1)
    picked_charge = jnp.take(atom_charge, near_list) * live_mask
    own_block = jnp.concatenate([picked_pos, picked_charge[None, :], live_mask[None, :]], axis=0)
    lanes = -(-capacity // 128) * 128
    tile = jnp.pad(own_block, ((0, 3), (0, lanes - capacity)))
    gathered = gather_all(tile, sizes, 0)
    coeffs, gathered = lax.optimization_barrier((coeffs, gathered))
    all_blocks = gathered[:, :5, :capacity].transpose(1, 0, 2).reshape(5, devices * capacity)
    live_total = all_blocks.shape[1] // 4
    order = jnp.cumsum(all_blocks[4]) - 1.0
    target = jnp.where(all_blocks[4] > 0.5, order, float(live_total)).astype(jnp.int32)
    select = (target[:, None] == jnp.arange(live_total)[None, :]).astype(jnp.float32)
    charges = jnp.dot(all_blocks[:4], select, precision=lax.Precision.HIGHEST)

    y_share = v_local.shape[1]
    x_points = jnp.arange(extent).astype(jnp.float32)
    y_points = (gvec_id * y_share + jnp.arange(y_share)).astype(jnp.float32)
    x_value, x_slope = kernels(x_points, charges[0], extent)
    y_value, y_slope = kernels(y_points, charges[1], extent)
    z_value, z_slope = kernels(x_points, charges[2], extent)
    weights = jnp.array(kernel_weights, jnp.float32)
    scaled = (weights[:, None] * charges[3][None, :]).reshape(-1)
    depth = (scaled[None, :] * z_value).astype(jnp.bfloat16)
    field_total = slab_potential(x_value, y_value, depth, v_local)

    gvec_size = sizes[1]
    chunks = 2 if y_share % 32 == 0 else 1
    chunk = y_share // chunks

    def y_rows(step, part):
        owner = lax.rem(gvec_id + step + gvec_size, gvec_size)
        return lax.dynamic_slice_in_dim(cosines, owner * y_share + part * chunk, chunk, 0)

    def a_columns(step):
        owner = lax.rem(gvec_id + step, gvec_size)
        return lax.dynamic_slice_in_dim(cosines, owner * x_local, x_local, 1)

    def shift(value, step):
        return lax.ppermute(
            value, "gvec", [(at, (at + step) % gvec_size) for at in range(gvec_size)]
        )

    section_z = jnp.einsum(
        "naql,zl->naqz", coeffs, cosines, preferred_element_type=jnp.float32
    ).astype(jnp.bfloat16)

    def section_y(step, part):
        return jnp.einsum(
            "naqz,yq->nayz", section_z, y_rows(step, part), preferred_element_type=jnp.float32
        ).astype(jnp.bfloat16)

    arrived = [
        [shift(section_y(-step, part), -step) for step in range(1, gvec_size)]
        for part in range(chunks)
    ]
    moments = 0.0
    reals = []
    returned = []
    own_sections = [section_y(0, part) for part in range(chunks)]
    for part in range(chunks):
        window = slice(part * chunk, (part + 1) * chunk)
        held = [own_sections[part]] + arrived[part]
        real_space = sum(
            jnp.einsum("nayz,xa->nxyz", block, a_columns(step), preferred_element_type=jnp.float32)
            for step, block in enumerate(held)
        ).astype(jnp.bfloat16)
        applied = (field_total[None, :, window] * real_space.astype(jnp.float32)).astype(jnp.bfloat16)

        def back_x(step):
            return jnp.einsum(
                "nxyz,xa->nayz", applied, a_columns(step), preferred_element_type=jnp.float32
            ).astype(jnp.bfloat16)

        sent = [back_x(step) for step in range(1, gvec_size)]
        if part == chunks - 1:
            sent, reals = lax.optimization_barrier((sent, reals + [real_space]))
        else:
            reals.append(real_space)
        returned.append(
            [shift(block, step) for step, block in enumerate(sent, 1)] + [back_x(0)]
        )
    for part in range(chunks):
        window = slice(part * chunk, (part + 1) * chunk)
        for band in range(local_bands):
            moments = moments + weight[band] * slab_moments(
                x_value, x_slope, y_value[window], y_slope[window], reals[part][band]
            )
    embedding = jnp.sum(moments[0] * depth.astype(jnp.float32)) / cell_count
    force_terms = jnp.stack(
        [
            jnp.sum(moments[1] * z_value, axis=0),
            jnp.sum(moments[2] * z_value, axis=0),
            jnp.sum(moments[0] * z_slope, axis=0),
        ]
    )
    force_terms = force_terms * scaled[None, :]
    forces = -force_unit * jnp.sum(force_terms.reshape(3, len(kernel_weights), -1), axis=1)

    steps = list(range(-1, -gvec_size, -1)) + [0]
    back_two = sum(
        jnp.einsum("nayz,yq->naqz", block, y_rows(step, part), preferred_element_type=jnp.float32)
        for part in range(chunks)
        for step, block in zip(steps, returned[part])
    ).astype(jnp.bfloat16)
    mine = (jnp.arange(band_total)[None, :] == band_ids[:, None]).astype(jnp.float32)
    flat = jnp.concatenate([forces.reshape(-1), jnp.zeros((6,), jnp.float32), embedding[None]])
    tail_length = flat.shape[0] + 3 * local_bands
    flat = jnp.pad(flat, (0, 3 * local_bands + -tail_length % 1024)).reshape(-1, 128)
    weight_row = jnp.pad(weight, (0, -local_bands % 128))[None, :]
    waves_new, parts = tail(back_two, coeffs, cosines, weight_row, flat, 3 * live_total, sizes)
    parts = parts.reshape(devices, -1)
    lines = 3 * live_total + 7
    summed = jnp.sum(parts[:, :lines], axis=0)
    force_all = summed[: 3 * live_total].reshape(3, live_total)
    by_group = parts[:, lines : lines + 3 * local_bands].reshape(
        sizes[0], gvec_size, sizes[2], 3, local_bands
    )
    norms, inners, squares = by_group[:, :, :, 0], by_group[:, :, :, 1], by_group[:, :, :, 2]
    norm_all = jnp.sum(norms, axis=1)
    energy_all = jnp.sum(inners, axis=1) / norm_all
    own_all = jnp.where(norms > 0.0, inners / jnp.where(norms > 0.0, norms, 1.0), 0.0)
    shifted = energy_all[:, None] - own_all
    ratio_all = (jnp.sum(squares + shifted * shifted * norms, axis=1) / norm_all).reshape(-1)
    energy_all = energy_all.reshape(-1)
    energies = jnp.sum(mine * energy_all[None, :], axis=1)
    resid_ratio = jnp.sum(mine * ratio_all[None, :], axis=1)
    band_energy = jnp.sum(occupancy(jnp.arange(band_total), band_total) * energy_all) / band_total
    totals = jnp.concatenate([summed[3 * live_total : 3 * live_total + 7], band_energy[None]])
    start = lax.dynamic_slice(order, (me * capacity,), (capacity,))
    own_target = jnp.where(live_mask > 0.5, start, float(live_total)).astype(jnp.int32)
    slot_select = (own_target[None, :] == jnp.arange(live_total)[:, None]).astype(jnp.float32)
    slot_force = jnp.dot(force_all, slot_select, precision=lax.Precision.HIGHEST)
    atom_select = (near_list[:, None] == jnp.arange(atom_pos.shape[1])[None, :]).astype(jnp.float32)
    atom_force = jnp.dot(slot_force, atom_select, precision=lax.Precision.HIGHEST)
    return (waves_new, energies, resid_ratio, atom_force, totals)


def solution(mesh):
    sizes = (mesh.shape["band"], mesh.shape["gvec"], mesh.shape["dom"])
    return jax.shard_map(
        functools.partial(per_device, sizes),
        mesh=mesh,
        in_specs=(
            P(("band", "dom"), "gvec", None, None),
            P(None, "gvec", None),
            P(None, ("band", "gvec", "dom")),
            P(("band", "gvec", "dom")),
            P(("band", "gvec", "dom")),
            P(("band", "gvec", "dom")),
        ),
        out_specs=(
            P(("band", "dom"), "gvec", None, None),
            P(("band", "dom")),
            P(("band", "dom")),
            P(None, ("band", "gvec", "dom")),
            P(),
        ),
        check_vma=False,
    )
```

profile of v0, /device:TPU:0, one launch (start us, length us, event | category | flops | bytes accessed | tf_op | source)
XLA Modules:
  0.0 111.1 jit_solution(2819963752244273305)
XLA Ops:
  2.0 0.9 copy.55
  5.5 13.3 %gather_0.1 = f32[32,8,128]{2,1,0:T(8,128)} custom-call(f32[8,128]{1,0:T(8,128)} %select_maximum_fusion.2.x_ref), custom_call_target="tpu_custom_call" | custom-call | tf_op jit(solution)/shard_map/gather_0/pallas_call | solution.py:84
  21.1 2.6 %fusion.7 = bf16[64,128,128]{2,1,0:T(8,128)(2,1)S(1)} fusion(bf16[1,64,128,128]{3,2,1,0:T(8,128)(2,1)} %coeff_ref, f32[128]{0:T(128)S(1)} %compare_select_fusion.4, f32[128]{0:T(128)S(1)} %iota_convert_fusion, f32[128]{0:T(128)S(1)} %add_multiply_fusion.1), kind=kOutput, calls=%fused_computation.14 | convolution fusion | flops 269549568 | bytes 4195840 | tf_op jit(solution)/shard_map/naql,zl->naqz/dot_general | solution.py:410
  23.6 1.3 %fusion.57 = (f32[128,128]{1,0:T(8,128)}, f32[128,128]{1,0:T(8,128)}, f32[128,128]{1,0:T(8,128)}, f32[128,128]{1,0:T(8,128)}, f32[128,128]{1,0:T(8,128)S(1)}, /*...) fusion(f32[128]{0:T(128)S(1)} %get-tuple-element.45, ...), kind=kLoop, calls=%fused_computation.119 | loop fusion | flops 622592 | bytes 1083904 | tf_op jit(solution)/shard_map/mul | solution.py:35
  24.9 1.2 %fusion.11 = bf16[1,64,32,128]{3,2,1,0:T(8,128)(2,1)} fusion(bf16[64,128,128]{2,1,0:T(8,128)(2,1)S(1)} %fusion.7, bf16[128,128]{1,0:T(8,128)(2,1)S(1)} %get-tuple-element.83.table_ref, s32[]{:T(128)S(6)} %select_n.104), kind=kOutput, calls=%fused_computation.24 | convolution fusion | flops 67371008 | bytes 2629636 | tf_op jit(solution)/shard_map/naqz,yq->nayz/dot_general | solution.py:415
  26.1 1.1 %collective-permute-start = (bf16[1,64,32,128]{3,2,1,0:T(8,128)(2,1)}, bf16[1,64,32,128]{3,2,1,0:T(8,128)(2,1)}, u32[]{:S(2)}, u32[]{:S(2)}) collective-permute-start(bf16[1,64,32,128]{3,2,1,0:T(8,128)(2,1)} %fusion.11), channel_id=1, source_target_pairs={{0,4},{4,0},{1,5},{5,1},{2,6},{6,2},{3,7},{7,3},{8,12},{12,8},{9,1... | collective-permute-start | bytes 1572872 | tf_op jit(solution)/shard_map/ppermute | solution.py:406
  27.3 1.2 %fusion.13 = bf16[1,64,32,128]{3,2,1,0:T(8,128)(2,1)} fusion(bf16[64,128,128]{2,1,0:T(8,128)(2,1)S(1)} %fusion.7, bf16[128,128]{1,0:T(8,128)(2,1)S(1)} %get-tuple-element.83.table_ref, s32[]{:T(128)S(6)} %select_n.111), kind=kOutput, calls=%fused_computation.26 | convolution fusion | flops 67371008 | bytes 2629636 | tf_op jit(solution)/shard_map/naqz,yq->nayz/dot_general | solution.py:415
  31.8 1.7 %pad_maximum_fusion.2.xs_ref = f32[128,512]{1,0:T(8,128)} fusion(f32[128,128]{1,0:T(8,128)} %get-tuple-element.81, f32[128,128]{1,0:T(8,128)} %get-tuple-element.80, f32[128,128]{1,0:T(8,128)} %get-tuple-element.79, f32[128,128]{1,0:T(8,128)} %get-tuple-element.82), kind=kLoop, calls=%fused_computation.83 | loop fusion | flops 196608 | bytes 524288 | tf_op jit(solution)/shard_map/concatenate | solution.py:36
  33.5 1.7 %pad_maximum_fusion = (f32[128,512]{1,0:T(8,128)}, bf16[128,512]{1,0:T(8,128)(2,1)}) fusion(f32[128,128]{1,0:T(8,128)} %get-tuple-element.78, f32[128,128]{1,0:T(8,128)} %get-tuple-element.76, f32[128,128]{1,0:T(8,128)} %get-tuple-element.77, f32[128,128]{1,0:T(8,128)S(1)} %get-tuple-element.75, f32[128,128]{1,0:T(8,128)S(1)} %get-tuple-element.55, ...), kind=kLoop, calls=%fused_computation.81 | loop fusion | flops 524288 | bytes 919552 | tf_op jit(solution)/shard_map/concatenate | solution.py:36
  35.2 7.8 %slab_potential.1 = f32[128,64,128]{2,1,0:T(8,128)} custom-call(f32[128,512]{1,0:T(8,128)} %get-tuple-element.84.x_ref.xv_ref, f32[64,512]{1,0:T(8,128)} %pad_maximum_fusion.3.y_ref, bf16[128,512]{1,0:T(8,128)(2,1)} %get-tuple-element.85.depth_ref, bf16[128,64,128]{2,1,0:T(8,128)(2,1)} %local_ref.1), custom_call_target="tpu_custom_call" | custom-call | flops 4294967296 | bytes 6291456 | tf_op jit(solution)/shard_map/slab_potential/pallas_call | solution.py:119
  44.6 6.7 %collective-permute-done.2 = bf16[1,64,32,128]{3,2,1,0:T(8,128)(2,1)} collective-permute-done((bf16[1,64,32,128]{3,2,1,0:T(8,128)(2,1)}, bf16[1,64,32,128]{3,2,1,0:T(8,128)(2,1)}, u32[]{:S(2)}, u32[]{:S(2)}) %collective-permute-start.2) | collective-permute-done | bytes 524320 | tf_op jit(solution)/shard_map/ppermute | solution.py:406
  51.3 1.7 %fusion.26 = f32[128,32,128]{2,0,1:T(8,128)S(1)} fusion(bf16[64,32,128]{2,1,0:T(8,128)(2,1)} %bitcast.36, bf16[128,128]{1,0:T(8,128)(2,1)S(1)} %get-tuple-element.83.table_ref, s32[]{:T(128)S(6)} %select_n.104), kind=kOutput, calls=%fused_computation.38 | convolution fusion | flops 67108864 | bytes 2654212 | tf_op jit(solution)/shard_map/nayz,xa->nxyz/dot_general | solution.py:431
  53.0 1.5 %fusion.34 = f32[128,32,128]{2,0,1:T(8,128)S(1)} fusion(bf16[64,32,128]{2,1,0:T(8,128)(2,1)} %bitcast.22, bf16[128,128]{1,0:T(8,128)(2,1)S(1)} %get-tuple-element.83.table_ref, s32[]{:T(128)S(6)} %select_n.104), kind=kOutput, calls=%fused_computation.46 | convolution fusion | flops 67108864 | bytes 2654212 | tf_op jit(solution)/shard_map/nayz,xa->nxyz/dot_general | solution.py:431
  54.5 6.4 %fusion.2 = (bf16[128,32,128]{2,1,0:T(8,128)(2,1)S(1)}, bf16[128,32,128]{2,1,0:T(8,128)(2,1)}, bf16[128,32,128]{2,1,0:T(8,128)(2,1)S(1)}, bf16[128,32,128]{2,1,0:T(8,128)(2,1)}) fusion(f32[128,64,128]{2,1,0:T(8,128)S(1)} %copy-done.3, f32[128,32,128]{2,0,1:T(8,128)S(1)} %fusion.34, f32[128,32,128]{2,0,1:T(8,128)S(1)} %fusion.36, ...), kind=kLoop, calls=%fused_computation.7 | loop fusion | flops 5242880 | bytes 16777216 | tf_op jit(solution)/shard_map/convert_element_type | solution.py:434
  63.0 1.5 %collective-permute-start.3 = (bf16[1,64,32,128]{3,1,2,0:T(8,128)(2,1)S(1)}, bf16[1,64,32,128]{3,1,2,0:T(8,128)(2,1)S(1)}, u32[]{:S(2)}, u32[]{:S(2)}) collective-permute-start(bf16[1,64,32,128]{3,1,2,0:T(8,128)(2,1)S(1)} %fusion.15), channel_id=1, source_target_pairs={{0,4},{4,0},{1,5},{5,1},{2,6},{6,2},{3,7},{7,3},{8,12},{12,8},{9,1... | collective-permute-start | bytes 1572872 | tf_op jit(solution)/shard_map/ppermute | solution.py:406
  65.1 2.7 %fusion.20 = f32[128,64,128]{2,0,1:T(8,128)} fusion(bf16[64,32,128]{2,0,1:T(8,128)(2,1)S(1)} %convolution_convert_fusion, bf16[128,128]{1,0:T(8,128)(2,1)S(1)} %get-tuple-element.83.table_ref, s32[]{:T(128)S(6)} %select_n.112), kind=kOutput, calls=%fused_computation.34 | convolution fusion | flops 67108864 | bytes 4726788 | tf_op jit(solution)/shard_map/nayz,yq->naqz/dot_general | solution.py:468
  67.8 2.7 %fusion.30 = f32[128,64,128]{2,0,1:T(8,128)} fusion(bf16[64,32,128]{2,0,1:T(8,128)(2,1)S(1)} %convolution_convert_fusion.2, bf16[128,128]{1,0:T(8,128)(2,1)S(1)} %get-tuple-element.83.table_ref, s32[]{:T(128)S(6)} %select_n.110), kind=kOutput, calls=%fused_computation.42 | convolution fusion | flops 67108864 | bytes 4726788 | tf_op jit(solution)/shard_map/nayz,yq->naqz/dot_general | solution.py:468
  70.5 7.0 %slab_moments.2 = f32[3,128,512]{2,1,0:T(8,128)} custom-call(f32[128,512]{1,0:T(8,128)} %get-tuple-element.84.x_ref.xv_ref, f32[128,512]{1,0:T(8,128)} %pad_maximum_fusion.2.xs_ref, f32[32,512]{1,0:T(8,128)} %get-tuple-element.86.yv_ref, f32[32,512]{1,0:T(8,128)} %get-tuple-element.39.ys_ref, bf16[128,32,128]{2,1,0:T(8,128)(2,1)} %get-tuple-element.29), custom_call_target="tpu_custom_call" | custom-call | flops 3221225472 | bytes 1048576 | tf_op jit(solution)/shard_map/slab_moments/pallas_call | solution.py:160
  77.4 7.0 %slab_moments.3 = f32[3,128,512]{2,1,0:T(8,128)} custom-call(f32[128,512]{1,0:T(8,128)} %get-tuple-element.84.x_ref.xv_ref, f32[128,512]{1,0:T(8,128)} %pad_maximum_fusion.2.xs_ref, f32[32,512]{1,0:T(8,128)} %get-tuple-element.87.yv_ref, f32[32,512]{1,0:T(8,128)} %get-tuple-element.38.ys_ref, bf16[128,32,128]{2,1,0:T(8,128)(2,1)} %get-tuple-element.37), custom_call_target="tpu_custom_call" | custom-call | flops 3221225472 | bytes 1048576 | tf_op jit(solution)/shard_map/slab_moments/pallas_call | solution.py:160
  84.5 1.3 %add_multiply_fusion = f32[3,128,512]{2,1,0:T(8,128)S(1)} fusion(f32[3,128,512]{2,1,0:T(8,128)S(1)} %copy-done.4, f32[3,128,512]{2,1,0:T(8,128)} %slab_moments.3, f32[]{:T(128)} %div.94), kind=kLoop, calls=%fused_computation.33 | loop fusion | flops 393216 | bytes 2359300 | tf_op jit(solution)/shard_map/add | solution.py:452
  88.1 1.4 %copy-done.2 = f32[128,64,128]{2,0,1:T(8,128)S(1)} copy-done((f32[128,64,128]{2,0,1:T(8,128)S(1)}, f32[128,64,128]{2,0,1:T(8,128)}, u32[]{:S(2)}) %copy-start.2) | copy-done | bytes 4194328
  89.6 3.6 %fusion.back_ref = bf16[1,64,128,128]{3,2,1,0:T(8,128)(2,1)S(1)} fusion(f32[128,64,128]{2,0,1:T(8,128)S(1)} %copy-done.2, f32[128,64,128]{2,0,1:T(8,128)S(1)} %fusion.32, f32[128,64,128]{2,0,1:T(8,128)} %fusion.30, bf16[64,32,128]{2,0,1:T(8,128)(2,1)S(1)} %bitcast.173, bf16[128,128]{1,0:T(8,128)(2,1)S(1)} %get-tuple-element.83.table_ref, s32[]{:T(128)S(6)} %select_n.111), kind=kOutput, calls=%fused_computation.3 | convolution fusion | flops 71303168 | bytes 15212548 | tf_op jit(solution)/shard_map/nayz,yq->naqz/dot_general | solution.py:468
  93.2 12.4 %tail.1 = (bf16[1,64,128,128]{3,2,1,0:T(8,128)(2,1)S(1)}, f32[32,8,128]{2,1,0:T(8,128)S(1)}) custom-call(bf16[1,64,128,128]{3,2,1,0:T(8,128)(2,1)S(1)} %fusion.back_ref, bf16[1,64,128,128]{3,2,1,0:T(8,128)(2,1)S(1)} %copy-done.1, bf16[128,128]{1,0:T(8,128)(2,1)S(1)} %get-tuple-element.83.table_ref, f32[1,128]{1,0:T(1,128)S(1)} %pad_bitcast_fusion.weight_ref, ...), custom_call_target="tpu_custom_call" | custom-call | tf_op jit(solution)/shard_map/tail/pallas_call | solution.py:332
  109.8 1.3 %copy.154 = bf16[1,64,128,128]{3,2,1,0:T(8,128)(2,1)} copy(bf16[1,64,128,128]{3,2,1,0:T(8,128)(2,1)S(1)} %get-tuple-element.93) | data formatting | bytes 4194304
  (93 shorter events, 18.1 us)
Async XLA Ops:
  0.6 2.3 %copy-start = (f32[1024]{0:T(1024)S(1)}, f32[1024]{0:T(1024)}, u32[]{:S(2)}) copy-start(f32[1024]{0:T(1024)} %param.10) | copy-start | bytes 12292
  26.1 26.8 %collective-permute-start = (bf16[1,64,32,128]{3,2,1,0:T(8,128)(2,1)}, bf16[1,64,32,128]{3,2,1,0:T(8,128)(2,1)}, u32[]{:S(2)}, u32[]{:S(2)}) collective-permute-start(bf16[1,64,32,128]{3,2,1,0:T(8,128)(2,1)} %fusion.11), channel_id=1, source_target_pairs={{0,4},{4,0},{1,5},{5,1},{2,6},{6,2},{3,7},{7,3},{8,12},{12,8},{9,1... | collective-permute-start | bytes 1572872 | tf_op jit(solution)/shard_map/ppermute | solution.py:406
  28.5 22.8 %collective-permute-start.2 = (bf16[1,64,32,128]{3,2,1,0:T(8,128)(2,1)}, bf16[1,64,32,128]{3,2,1,0:T(8,128)(2,1)}, u32[]{:S(2)}, u32[]{:S(2)}) collective-permute-start(bf16[1,64,32,128]{3,2,1,0:T(8,128)(2,1)} %fusion.13), channel_id=1, source_target_pairs={{0,4},{4,0},{1,5},{5,1},{2,6},{6,2},{3,7},{7,3},{8,12},{12,8},{9,1... | collective-permute-start | bytes 1572872 | tf_op jit(solution)/shard_map/ppermute | solution.py:406
  29.5 0.8 copy-start.12
  43.0 0.9 copy-start.5
  51.3 3.2 %copy-start.3 = (f32[128,64,128]{2,1,0:T(8,128)S(1)}, f32[128,64,128]{2,1,0:T(8,128)}, u32[]{:S(2)}) copy-start(f32[128,64,128]{2,1,0:T(8,128)} %slab_potential.1) | copy-start | bytes 12582916
  63.0 25.1 %collective-permute-start.3 = (bf16[1,64,32,128]{3,1,2,0:T(8,128)(2,1)S(1)}, bf16[1,64,32,128]{3,1,2,0:T(8,128)(2,1)S(1)}, u32[]{:S(2)}, u32[]{:S(2)}) collective-permute-start(bf16[1,64,32,128]{3,1,2,0:T(8,128)(2,1)S(1)} %fusion.15), channel_id=1, source_target_pairs={{0,4},{4,0},{1,5},{5,1},{2,6},{6,2},{3,7},{7,3},{8,12},{12,8},{9,1... | collective-permute-start | bytes 1572872 | tf_op jit(solution)/shard_map/ppermute | solution.py:406
  64.5 22.9 %collective-permute-start.1 = (bf16[1,64,32,128]{3,1,2,0:T(8,128)(2,1)S(1)}, bf16[1,64,32,128]{3,1,2,0:T(8,128)(2,1)S(1)}, u32[]{:S(2)}, u32[]{:S(2)}) collective-permute-start(bf16[1,64,32,128]{3,1,2,0:T(8,128)(2,1)S(1)} %fusion.14), channel_id=1, source_target_pairs={{0,4},{4,0},{1,5},{5,1},{2,6},{6,2},{3,7},{7,3},{8,12},{12,8},{9,1... | collective-permute-start | bytes 1572872 | tf_op jit(solution)/shard_map/ppermute | solution.py:406
  77.4 7.0 %copy-start.4 = (f32[3,128,512]{2,1,0:T(8,128)S(1)}, f32[3,128,512]{2,1,0:T(8,128)}, u32[]{:S(2)}) copy-start(f32[3,128,512]{2,1,0:T(8,128)} %slab_moments.2) | copy-start | bytes 2359300
  84.4 1.4 %copy-start.6 = (bf16[128,512]{1,0:T(8,128)(2,1)S(1)}, bf16[128,512]{1,0:T(8,128)(2,1)}, u32[]{:S(2)}) copy-start(bf16[128,512]{1,0:T(8,128)(2,1)} %get-tuple-element.85.depth_ref) | copy-start | bytes 393220
  84.4 1.4 %copy-start.7 = (f32[128,128]{1,0:T(8,128)S(1)}, f32[128,128]{1,0:T(8,128)}, u32[]{:S(2)}) copy-start(f32[128,128]{1,0:T(8,128)} %get-tuple-element.51) | copy-start | bytes 196612
  84.5 1.4 %copy-start.8 = (f32[128,128]{1,0:T(8,128)S(1)}, f32[128,128]{1,0:T(8,128)}, u32[]{:S(2)}) copy-start(f32[128,128]{1,0:T(8,128)} %get-tuple-element.52) | copy-start | bytes 196612
  84.5 1.4 %copy-start.9 = (f32[128,128]{1,0:T(8,128)S(1)}, f32[128,128]{1,0:T(8,128)}, u32[]{:S(2)}) copy-start(f32[128,128]{1,0:T(8,128)} %get-tuple-element.53) | copy-start | bytes 196612
  84.5 1.4 %copy-start.10 = (f32[128,128]{1,0:T(8,128)S(1)}, f32[128,128]{1,0:T(8,128)}, u32[]{:S(2)}) copy-start(f32[128,128]{1,0:T(8,128)} %get-tuple-element.54) | copy-start | bytes 196612
  87.4 2.2 %copy-start.2 = (f32[128,64,128]{2,0,1:T(8,128)S(1)}, f32[128,64,128]{2,0,1:T(8,128)}, u32[]{:S(2)}) copy-start(f32[128,64,128]{2,0,1:T(8,128)} %fusion.20) | copy-start | bytes 12582916
  89.6 3.6 %copy-start.1 = (bf16[1,64,128,128]{3,2,1,0:T(8,128)(2,1)S(1)}, bf16[1,64,128,128]{3,2,1,0:T(8,128)(2,1)}, u32[]{:S(2)}) copy-start(bf16[1,64,128,128]{3,2,1,0:T(8,128)(2,1)} %coeff_ref) | copy-start | bytes 6291460
  93.2 12.7 %copy-start.11 = (s32[16]{0:T(128)S(1)}, s32[16]{0:T(128)}, u32[]{:S(2)}) copy-start(s32[16]{0:T(128)} %param.11) | copy-start | bytes 196
where the time goes:
time: 112 us; the launch traced here: 111 us
  Pallas kernels  47.5 us (42%)
  matrix products  23 us (21%)
  other arithmetic  18.6 us (17%)
  local copies, waits for them, and re-layouts  8.13 us (7%)
  waiting for transfers between devices  6.7 us (6%)
  starting transfers between devices  4.11 us (4%)
  between operations  3.05 us (3%)
    pallas_call x2, Pallas kernels, slab_moments(): pl.pallas_call(force_kernel, grid=(x_total // rows,), out_shape=jax.Shape...  14 us
    pallas_call x1, Pallas kernels, gather_all(): pl.pallas_call(functools.partial(gather_kernel, sizes), out_shape=jax.Sha...  13.3 us
    pallas_call x1, Pallas kernels, tail(): pl.pallas_call(functools.partial(tail_kernel, sizes, base), out_shape=(ja...  12.4 us
    dot_general x4, matrix products, per_device(): jnp.einsum('nayz,yq->naqz', block, y_rows(step, part), preferred_element_...  9.74 us
    pallas_call x1, Pallas kernels, slab_potential(): pl.pallas_call(potential_kernel, grid=(x_total // rows,), out_shape=jax.S...  7.83 us
    ppermute x4, waiting for transfers between devices, shift(): lax.ppermute(value, 'gvec', [(at, (at + step) % gvec_size) for at in rang...  6.7 us
    convert_element_type x1, other arithmetic, per_device(): (field_total[None, :, window] * real_space.astype(jnp.float32)).astype(jn...  6.38 us
    unnamed x32, local copies, waits for them, and re-layouts  4.59 us
  transfers between devices with their start and end apart: 4, of which 1 were waited for; matrix products, arithmetic and copies ran while one was open for 16% of the time, Pallas kernels for 20%

commit v1 on v0

v1 whole, which is shorter than its diff:
```python
import functools

import jax
import jax.numpy as jnp
import numpy as np
from jax import lax
from jax.experimental import pallas as pl
from jax.experimental.pallas import tpu as pltpu
from jax.sharding import PartitionSpec as P

sigma_fractions = (1.0 / 32.0, 1.0 / 16.0, 1.0 / 8.0, 1.0 / 4.0)
kernel_weights = (1.0, 0.5, 0.25, 0.125)
force_unit = 1.0 / 4096.0
step_size = 0.5
MESH = pl.DeviceIdType.MESH
F32 = jnp.float32
BF16 = jnp.bfloat16
HIGH = lax.Precision.HIGHEST


def cosine_table(length):
    points = np.arange(length).astype(np.float32)
    angles = np.float32(np.pi) * (points[:, None] + np.float32(0.5)) * points[None, :] / np.float32(length)
    scales = np.where(points == 0.0, np.sqrt(1.0 / length), np.sqrt(2.0 / length)).astype(np.float32)
    return (np.cos(angles.astype(np.float64)).astype(np.float32) * scales[None, :]).astype(jnp.bfloat16)


def constant_tables(length):
    cosines = cosine_table(length)
    zero = np.zeros_like(cosines)
    pair = np.stack([cosines, cosines.T])
    diagonal = np.stack(
        [np.block([[cosines.T, zero], [zero, cosines.T]]), np.block([[cosines, zero], [zero, cosines]])]
    )
    return pair, diagonal


def group_tables(sizes):
    band_size, gvec_size, dom_size = sizes
    total = band_size * gvec_size * dom_size
    at = np.arange(total)
    group = (at // (gvec_size * dom_size)) * dom_size + at % dom_size
    same = (group[:, None] == group[None, :]).astype(np.float32)
    before = (at[None, :] < at[:, None]).astype(np.float32)
    return np.stack([same, before]), group.astype(np.float32)[:, None]


def dot(left, right):
    return jnp.dot(left, right, preferred_element_type=F32)


def total_of(value):
    return jnp.sum(jnp.sum(value, axis=0, keepdims=True), axis=1, keepdims=True)


def iota(shape, axis):
    return lax.broadcasted_iota(jnp.int32, shape, axis)


def step_kernel(
    sizes, plan,
    near_ref, live_ref, pos_ref, charge_ref, cos_ref, diag_ref, group_ref, band_ref, coeff_hbm, local_hbm,
    waves_ref, force_out, misc_ref,
    coeff_ref, local_ref, stage_ref, sect_ref, held_ref, field_ref, dens_ref, going_ref, back_ref,
    image_ref, recip_ref, moment_ref, row_ref, rows_ref, tile_ref, tiles_ref, last_ref, lasts_ref,
    xg_ref, xh_ref, yg_ref, y_ref, depth_ref, zg_ref, zh_ref, scale_ref, place_ref, proj_ref,
    load_sem, local_sem, own_sem, fsend, frecv, bsend, brecv, csend, crecv,
):
    band_size, gvec_size, dom_size = sizes
    total = band_size * gvec_size * dom_size
    x_local, extent, y_share, cap, live_total, atoms = plan
    band_id, gvec_id, dom_id = lax.axis_index("band"), lax.axis_index("gvec"), lax.axis_index("dom")
    me = (band_id * gvec_size + gvec_id) * dom_size + dom_id
    band_total = band_size * dom_size
    width = len(kernel_weights) * live_total
    cells = float(extent**3)
    wave_step = np.float32(np.pi / extent)
    y_chunk = 16 if y_share % 16 == 0 else y_share
    chunks = y_share // y_chunk
    piece = 16 if x_local % 16 == 0 else x_local
    pieces = x_local // piece
    barrier = pltpu.get_barrier_semaphore()

    def peer_of(step):
        outer = step // gvec_size
        return (
            lax.rem(band_id + outer // dom_size, band_size),
            lax.rem(gvec_id + step % gvec_size, gvec_size),
            lax.rem(dom_id + outer % dom_size, dom_size),
        )

    def greet(step, carry):
        pl.semaphore_signal(barrier, inc=1, device_id=peer_of(step), device_id_type=MESH)
        return carry

    lax.fori_loop(1, total, greet, 0)

    def load_of(part):
        window = pl.ds(part * piece, piece)
        return pltpu.make_async_copy(coeff_hbm.at[0, window], coeff_ref.at[window], load_sem.at[part])

    for part in range(pieces):
        load_of(part).start()
    local_copy = pltpu.make_async_copy(local_hbm, local_ref, local_sem)
    local_copy.start()

    def broadcast(kind, src, dst):
        def copy_of(step):
            return pltpu.make_async_remote_copy(
                src_ref=src, dst_ref=dst.at[me],
                send_sem=csend.at[kind, step], recv_sem=crecv.at[kind, step],
                device_id=peer_of(step), device_id_type=MESH,
            )

        def send(step, carry):
            copy_of(step).start()
            return carry

        def finish(step, carry):
            copy_of(step).wait()
            return carry

        def start():
            lax.fori_loop(1, total, send, 0)

        def wait(first, stop):
            lax.fori_loop(first, stop, finish, 0)

        return start, wait

    lanes = row_ref.shape[1]
    lane = iota((1, lanes), 1)
    near_row = jnp.full((1, lanes), -1, jnp.int32)
    for quantity in range(4):
        for slot in range(cap):
            near_row = jnp.where(lane == quantity * cap + slot, near_ref[slot], near_row)
    live = live_ref[0]
    chosen = (iota((atoms, lanes), 0) == near_row).astype(F32)
    picked_pos = jnp.dot(pos_ref[...], chosen, precision=HIGH, preferred_element_type=F32)
    picked_charge = jnp.dot(charge_ref[...], chosen, precision=HIGH, preferred_element_type=F32)
    row = jnp.zeros((1, lanes), F32)
    for quantity in range(3):
        part = (lane >= quantity * cap) & (lane < (quantity + 1) * cap)
        row = jnp.where(part, picked_pos[quantity : quantity + 1], row)
    part = (lane >= 3 * cap) & (lane < 3 * cap + live) & (lane < 4 * cap)
    row = jnp.where(part, picked_charge, row)
    row = jnp.where(lane == 4 * cap, live.astype(F32), row)
    row_ref[...] = row
    rows_ref[me] = row

    group = piece

    def forward(index, carry):
        load_of(index).wait()
        for pair in range(group // 2):
            first = index * group + 2 * pair
            both = jnp.concatenate([coeff_ref[first], coeff_ref[first + 1]], axis=1)
            section = dot(both, diag_ref[0]).astype(BF16)
            result = dot(cos_ref[0], section)
            stage_ref[pl.ds(2 * pair * extent, extent)] = result[:, :extent]
            stage_ref[pl.ds((2 * pair + 1) * extent, extent)] = result[:, extent:]
        window = pl.ds(pl.multiple_of(index * group, group), group)

        def spread(outer, inner_carry):
            for inner in range(8):
                y = outer * 8 + inner
                sect_ref[y, window] = stage_ref[pl.ds(y, group, stride=extent)].astype(BF16)
            return inner_carry

        lax.fori_loop(0, extent // 8, spread, 0)
        return carry

    lax.fori_loop(0, pieces, forward, 0)
    pl.semaphore_wait(barrier, total - 1)

    start_rows, wait_rows = broadcast(0, row_ref, rows_ref)
    start_rows()

    def gvec_peer(step):
        return (band_id, lax.rem(gvec_id + step, gvec_size), dom_id)

    def forward_copy(step, chunk):
        owner = lax.rem(gvec_id + step, gvec_size)
        return pltpu.make_async_remote_copy(
            src_ref=sect_ref.at[pl.ds(owner * y_share + chunk * y_chunk, y_chunk)],
            dst_ref=held_ref.at[gvec_id, pl.ds(chunk * y_chunk, y_chunk)],
            send_sem=fsend.at[step, chunk], recv_sem=frecv.at[step, chunk],
            device_id=gvec_peer(step), device_id_type=MESH,
        )

    for chunk in range(chunks):
        for step in range(1, gvec_size):
            forward_copy(step, chunk).start()
    own_copy = pltpu.make_async_copy(
        sect_ref.at[pl.ds(gvec_id * y_share, y_share)], held_ref.at[gvec_id], own_sem.at[0]
    )
    own_copy.start()

    local_copy.wait()
    x_block = 16

    def turn_local(index, carry):
        window = pl.ds(pl.multiple_of(index * x_block, x_block), x_block)
        stage_ref[pl.ds(0, x_block * y_share)] = (
            local_ref[window].astype(F32).reshape(x_block * y_share, extent)
        )

        def turn(outer, inner_carry):
            for inner in range(8):
                y = outer * 8 + inner
                field_ref[y, window] = stage_ref[pl.ds(y, x_block, stride=y_share)]
            return inner_carry

        lax.fori_loop(0, y_share // 8, turn, 0)
        return carry

    lax.fori_loop(0, extent // x_block, turn_local, 0)

    wait_rows(1, total)
    rows = rows_ref[:, 0, :]
    count = rows[:, 4 * cap : 4 * cap + 1]
    count_wide = jnp.broadcast_to(count, (total, live_total))
    offset = jnp.dot(group_ref[1], count_wide, precision=HIGH, preferred_element_type=F32)
    order = iota((total, live_total), 1).astype(F32)
    holds = ((order >= offset) & (order < offset + count_wide)).astype(F32)
    slot_at = jnp.sum(holds * (order - offset), axis=0, keepdims=True)
    spread_rows = lax.dot_general(
        rows, holds, (((0,), (0,)), ((), ())), precision=HIGH, preferred_element_type=F32
    )
    here = (iota((cap, live_total), 0).astype(F32) == slot_at).astype(F32)
    centre = [
        jnp.sum(spread_rows[k * cap : (k + 1) * cap] * here, axis=0, keepdims=True) for k in range(4)
    ]
    mine = (iota((total, 1), 0) == me).astype(F32)
    own_offset = jnp.sum(mine * offset[:, :1], axis=0, keepdims=True)
    place_ref[...] = jnp.broadcast_to(own_offset, place_ref.shape)

    x_points = iota((extent, live_total), 0).astype(F32)
    y_points = (iota((y_share, live_total), 0) + gvec_id * y_share).astype(F32)
    for k, fraction in enumerate(sigma_fractions):
        exponent = 0.5 / (extent * fraction) ** 2
        window = slice(k * live_total, (k + 1) * live_total)
        scaled = kernel_weights[k] * centre[3]
        scale_ref[:, window] = scaled
        away = x_points - centre[0]
        value = jnp.exp(-exponent * away * away)
        xg_ref[:, window] = value
        xh_ref[:, window] = 2.0 * exponent * away * value
        away = y_points - centre[1]
        value = jnp.exp(-exponent * away * away)
        slope = 2.0 * exponent * away * value
        yg_ref[:, window] = value
        for part in range(live_total // 128):
            y_ref[0, k * live_total // 128 + part] = value[:, part * 128 : (part + 1) * 128]
            y_ref[1, k * live_total // 128 + part] = slope[:, part * 128 : (part + 1) * 128]
        away = x_points - centre[2]
        value = jnp.exp(-exponent * away * away)
        depth_ref[:, window] = (scaled * value).astype(BF16)
        zg_ref[:, window] = value.astype(BF16)
        zh_ref[:, window] = (2.0 * exponent * away * value).astype(BF16)

    block = min(width, 512)

    def add_field(y, carry):
        value = None
        for part in range(width // block):
            window = slice(part * block, (part + 1) * block)
            plane = (xg_ref[:, window] * yg_ref[pl.ds(y, 1), window]).astype(BF16)
            term = lax.dot_general(
                plane, depth_ref[:, window], (((1,), (1,)), ((), ())), preferred_element_type=F32
            )
            value = term if value is None else value + term
        field_ref[y] += value.astype(BF16).astype(F32)
        return carry

    lax.fori_loop(0, y_share, add_field, 0)

    def back_copy(step, chunk, part):
        owner = lax.rem(gvec_id + step, gvec_size)
        return pltpu.make_async_remote_copy(
            src_ref=going_ref.at[chunk, pl.ds(owner * x_local + part * piece, piece)],
            dst_ref=back_ref.at[gvec_id, chunk, pl.ds(part * piece, piece)],
            send_sem=bsend.at[step, chunk, part], recv_sem=brecv.at[step, chunk, part],
            device_id=gvec_peer(step), device_id_type=MESH,
        )

    def own_back(chunk):
        return pltpu.make_async_copy(
            going_ref.at[chunk, pl.ds(gvec_id * x_local, x_local)],
            back_ref.at[gvec_id, chunk], own_sem.at[1 + chunk],
        )

    own_copy.wait()

    def middle(chunk, carry):
        for step in range(1, gvec_size):
            forward_copy(step, chunk).wait_recv()
        for pair in range(y_chunk // 2):
            first = chunk * y_chunk + 2 * pair
            both = jnp.concatenate(
                [
                    jnp.concatenate([held_ref[source, first + side] for source in range(gvec_size)], axis=0)
                    for side in range(2)
                ],
                axis=1,
            )
            wide = dot(cos_ref[0], both).astype(BF16).astype(F32)
            square = (wide * wide).astype(BF16)
            dens_ref[first] = square[:, :extent]
            dens_ref[first + 1] = square[:, extent:]
            fields = jnp.concatenate([field_ref[first], field_ref[first + 1]], axis=1)
            result = dot(cos_ref[1], (fields * wide).astype(BF16))
            stage_ref[pl.ds(2 * pair * extent, extent)] = result[:, :extent]
            stage_ref[pl.ds((2 * pair + 1) * extent, extent)] = result[:, extent:]

        def spread(outer, inner_carry):
            for inner in range(8):
                a = outer * 8 + inner
                going_ref[chunk, a] = stage_ref[pl.ds(a, y_chunk, stride=extent)].astype(BF16)
            return inner_carry

        lax.fori_loop(0, extent // 8, spread, 0)
        for part in range(pieces):
            for step in range(1, gvec_size):
                back_copy(step, chunk, part).start()
        own_back(chunk).start()
        return carry

    lax.fori_loop(0, chunks, middle, 0)

    q_wave = iota((extent, extent), 0).astype(F32) * wave_step
    l_wave = iota((extent, extent), 1).astype(F32) * wave_step
    plane_kinetic = 0.5 * (q_wave * q_wave + l_wave * l_wave)
    moment_ref[...] = jnp.zeros_like(moment_ref)

    def x_wave_of(a):
        return jnp.full((1, 1), gvec_id * x_local + a, jnp.int32).astype(F32) * wave_step

    def coefficients(index, carry):
        zero, one, two = 0.0, 0.0, 0.0
        for inner in range(4):
            a = index * 4 + inner
            wide = coeff_ref[a].astype(F32)
            x_wave = x_wave_of(a)
            square = wide * wide
            by_x = square * x_wave
            zero, one, two = zero + square, one + by_x, two + by_x * x_wave
            recip_ref[a] = step_size / (1.0 + 0.5 * x_wave * x_wave + plane_kinetic)
        moment_ref[0] += zero
        moment_ref[1] += one
        moment_ref[2] += two
        return carry

    lax.fori_loop(0, x_local // 4, coefficients, 0)
    group_id = band_id * dom_size + dom_id
    shifted = jnp.full((1, 1), group_id, jnp.int32).astype(F32) - 0.5 * band_total
    weight = 2.0 / (1.0 + jnp.exp(shifted / (0.125 * band_total)))
    terms = (
        moment_ref[2],
        moment_ref[0] * q_wave * q_wave,
        moment_ref[0] * l_wave * l_wave,
        moment_ref[1] * q_wave,
        moment_ref[1] * l_wave,
        moment_ref[0] * q_wave * l_wave,
    )
    stress = [weight * total_of(term) / cells for term in terms]

    y_block = 16 if y_share % 16 == 0 else y_share
    x_part = 32

    def project(index, carry):
        at = pl.ds(pl.multiple_of(index * 128, 128), 128)
        tables = jnp.concatenate([zg_ref[:, at], zh_ref[:, at]], axis=1)
        sums = [jnp.zeros((1, 128), F32) for _ in range(4)]
        for x_at in range(extent // x_part):
            x_window = pl.ds(x_at * x_part, x_part)

            def over_y(outer, accs):
                along, slope, deep = accs
                left = dens_ref[pl.ds(outer * y_block, y_block), x_window].reshape(y_block * x_part, extent)
                result = dot(left, tables)
                for inner in range(y_block):
                    y = outer * y_block + inner
                    rows_at = slice(inner * x_part, (inner + 1) * x_part)
                    value, derivative = y_ref[0, index, pl.ds(y, 1)], y_ref[1, index, pl.ds(y, 1)]
                    along = along + result[rows_at, :128] * value
                    slope = slope + result[rows_at, :128] * derivative
                    deep = deep + result[rows_at, 128:] * value
                return along, slope, deep

            start = tuple(jnp.zeros((x_part, 128), F32) for _ in range(3))
            along, slope, deep = lax.fori_loop(0, y_share // y_block, over_y, start)
            value, derivative = xg_ref[x_window, at], xh_ref[x_window, at]
            for at_sum, term in enumerate((derivative * along, value * slope, value * deep, value * along)):
                sums[at_sum] = sums[at_sum] + jnp.sum(term, axis=0, keepdims=True)
        for at_sum in range(4):
            proj_ref[at_sum : at_sum + 1, at] = sums[at_sum] * scale_ref[:, at]
        return carry

    lax.fori_loop(0, width // 128, project, 0)
    folded = jnp.zeros((4, live_total), F32)
    for k in range(len(kernel_weights)):
        folded = folded + proj_ref[:, k * live_total : (k + 1) * live_total]
    tile_ref[0:3] = (-force_unit * weight) * folded[0:3]
    embedding = weight * jnp.sum(folded[3:4], axis=1, keepdims=True) / cells
    line = jnp.zeros((1, live_total), F32)
    tile_lane = iota((1, live_total), 1)
    for at, value in enumerate(stress + [embedding]):
        line = jnp.where(tile_lane == at, value, line)
    tile_ref[3:4] = line
    tiles_ref[me] = tile_ref[...]
    start_tiles, wait_tiles = broadcast(1, tile_ref, tiles_ref)
    start_tiles()

    for chunk in range(chunks):
        own_back(chunk).wait()
    norms, inners, squares = [], [], []
    for part in range(pieces):
        for chunk in range(chunks):
            for step in range(1, gvec_size):
                back_copy(step, chunk, part).wait_recv()

        def image_of(index, carry):
            norm, inner = carry
            for pair in range(2):
                first = part * piece + 4 * index + 2 * pair
                both = jnp.concatenate(
                    [
                        jnp.concatenate(
                            [
                                back_ref[source, chunk, first + side]
                                for source in range(gvec_size)
                                for chunk in range(chunks)
                            ],
                            axis=0,
                        )
                        for side in range(2)
                    ],
                    axis=1,
                )
                section = dot(cos_ref[1], both).astype(BF16)
                waves = dot(section, diag_ref[1])
                for side in range(2):
                    a = first + side
                    wide = coeff_ref[a].astype(F32)
                    x_wave = x_wave_of(a)
                    image = (0.5 * x_wave * x_wave + plane_kinetic) * wide
                    image = image + waves[:, side * extent : (side + 1) * extent]
                    image_ref[a] = image
                    norm = norm + jnp.sum((wide * wide).reshape(-1, 8, extent), axis=0)
                    inner = inner + jnp.sum((wide * image).reshape(-1, 8, extent), axis=0)
            return norm, inner

        empty = jnp.zeros((8, extent), F32)
        norm, inner = lax.fori_loop(0, piece // 4, image_of, (empty, empty))
        norm, inner = total_of(norm), total_of(inner)
        filled = norm > 0.0
        energy = jnp.where(filled, inner / jnp.where(filled, norm, 1.0), 0.0)

        def residual_of(index, square):
            for side in range(4):
                a = part * piece + 4 * index + side
                wide = coeff_ref[a].astype(F32)
                image = image_ref[a]
                residual = image - energy * wide
                square = square + jnp.sum((residual * residual).reshape(-1, 8, extent), axis=0)
                image_ref[a] = wide - image * recip_ref[a]
            return square

        square = total_of(lax.fori_loop(0, piece // 4, residual_of, empty))
        norms.append(norm)
        inners.append(inner)
        squares.append(square)

    def merged(parts):
        norm = sum(part[0] for part in parts)
        inner = sum(part[1] for part in parts)
        filled = norm > 0.0
        energy = jnp.where(filled, inner / jnp.where(filled, norm, 1.0), 0.0)
        square = 0.0
        for part_norm, part_inner, part_square in parts:
            filled = part_norm > 0.0
            part_energy = jnp.where(filled, part_inner / jnp.where(filled, part_norm, 1.0), 0.0)
            away = part_energy - energy
            square = square + part_square + away * away * part_norm
        return norm, inner, square

    own = merged(list(zip(norms, inners, squares)))
    last_lane = iota(last_ref.shape, 1)
    last = jnp.zeros(last_ref.shape, F32)
    for at, value in enumerate(own):
        last = jnp.where(last_lane == at, value, last)
    last_ref[...] = last
    lasts_ref[me] = last
    start_last, wait_last = broadcast(2, last_ref, lasts_ref)
    start_last()
    wait_last(1, gvec_size)
    parts = []
    for source in range(gvec_size):
        other = lasts_ref[(band_id * gvec_size + source) * dom_size + dom_id]
        parts.append(tuple(other[:, at : at + 1] for at in range(3)))
    norm, inner, square = merged(parts)
    energy = inner / norm

    def update(index, carry):
        for side in range(4):
            a = index * 4 + side
            wide = coeff_ref[a].astype(F32)
            waves_ref[0, a] = (image_ref[a] + energy * (wide * recip_ref[a])).astype(BF16)
        return carry

    lax.fori_loop(0, x_local // 4, update, 0)

    wait_tiles(1, total)
    summed = tiles_ref[0]
    for source in range(1, total):
        summed = summed + tiles_ref[source]
    slot_lanes = (iota((live_total, 128), 0).astype(F32) - place_ref[0:1, 0:1]) == iota(
        (live_total, 128), 1
    ).astype(F32)
    slot_lanes = slot_lanes & (iota((live_total, 128), 1) < live)
    slot_force = jnp.dot(summed, slot_lanes.astype(F32), precision=HIGH, preferred_element_type=F32)
    near_column = jnp.full((128, 1), -1, jnp.int32)
    for slot in range(cap):
        near_column = jnp.where(iota((128, 1), 0) == slot, near_ref[slot], near_column)
    at_atom = (iota((128, atoms), 1) == near_column).astype(F32)
    atom_force = jnp.dot(slot_force, at_atom, precision=HIGH, preferred_element_type=F32)
    force_out[...] = atom_force[0:3]

    wait_last(gvec_size, total)
    lasts = lasts_ref[:, 0, :]
    both = jnp.dot(group_ref[0], lasts, precision=HIGH, preferred_element_type=F32)
    band_energy = both[:, 1:2] / both[:, 0:1]
    occupied = 2.0 / (1.0 + jnp.exp((band_ref[...] - 0.5 * band_total) / (0.125 * band_total)))
    band_sum = jnp.sum(occupied * band_energy, axis=0, keepdims=True) / float(gvec_size * band_total)
    misc_lane = iota((1, 128), 1)
    misc_ref[0:1] = jnp.broadcast_to(energy, (1, 128))
    misc_ref[1:2] = jnp.broadcast_to(square / norm, (1, 128))
    misc_ref[2:3] = jnp.where(misc_lane == 7, band_sum, summed[3:4, :128])
    misc_ref[3:8] = jnp.zeros((5, 128), F32)

    for step in range(1, gvec_size):
        for chunk in range(chunks):
            forward_copy(step, chunk).wait_send()
            for part in range(pieces):
                back_copy(step, chunk, part).wait_send()


def per_device(sizes, coeffs, v_local, atom_pos, atom_charge, near_list, live_count):
    gvec_size = sizes[1]
    total = sizes[0] * sizes[1] * sizes[2]
    local_bands, x_local, extent, _ = coeffs.shape
    assert local_bands == 1
    y_share = v_local.shape[1]
    cap = near_list.shape[0]
    atoms = atom_pos.shape[1]
    live_total = total * cap // 4
    width = len(kernel_weights) * live_total
    y_chunk = 16 if y_share % 16 == 0 else y_share
    chunks = y_share // y_chunk
    piece = 16 if x_local % 16 == 0 else x_local
    pieces = x_local // piece
    lanes = -(-(4 * cap + 1) // 128) * 128
    pair, diagonal = constant_tables(extent)
    groups, bands = group_tables(sizes)
    vmem = pl.BlockSpec(memory_space=pltpu.VMEM)
    smem = pl.BlockSpec(memory_space=pltpu.SMEM)
    hbm = pl.BlockSpec(memory_space=pl.ANY)
    plan = (x_local, extent, y_share, cap, live_total, atoms)
    deep = max(piece, y_chunk, 16)
    dma = pltpu.SemaphoreType.DMA
    waves_new, atom_force, misc = pl.pallas_call(
        functools.partial(step_kernel, sizes, plan),
        out_shape=(
            jax.ShapeDtypeStruct(coeffs.shape, BF16),
            jax.ShapeDtypeStruct((3, atoms), F32),
            jax.ShapeDtypeStruct((8, 128), F32),
        ),
        in_specs=[smem, smem, vmem, vmem, vmem, vmem, vmem, vmem, hbm, hbm],
        out_specs=(vmem, vmem, vmem),
        scratch_shapes=[
            pltpu.VMEM((x_local, extent, extent), BF16),
            pltpu.VMEM(v_local.shape, BF16),
            pltpu.VMEM((deep * extent, extent), F32),
            pltpu.VMEM((extent, x_local, extent), BF16),
            pltpu.VMEM((gvec_size, y_share, x_local, extent), BF16),
            pltpu.VMEM((y_share, extent, extent), F32),
            pltpu.VMEM((y_share, extent, extent), BF16),
            pltpu.VMEM((chunks, extent, y_chunk, extent), BF16),
            pltpu.VMEM((gvec_size, chunks, x_local, y_chunk, extent), BF16),
            pltpu.VMEM((x_local, extent, extent), F32),
            pltpu.VMEM((x_local, extent, extent), F32),
            pltpu.VMEM((3, extent, extent), F32),
            pltpu.VMEM((1, lanes), F32),
            pltpu.VMEM((total, 1, lanes), F32),
            pltpu.VMEM((4, live_total), F32),
            pltpu.VMEM((total, 4, live_total), F32),
            pltpu.VMEM((1, 128), F32),
            pltpu.VMEM((total, 1, 128), F32),
            pltpu.VMEM((extent, width), F32),
            pltpu.VMEM((extent, width), F32),
            pltpu.VMEM((y_share, width), F32),
            pltpu.VMEM((2, width // 128, y_share, 128), F32),
            pltpu.VMEM((extent, width), BF16),
            pltpu.VMEM((extent, width), BF16),
            pltpu.VMEM((extent, width), BF16),
            pltpu.VMEM((1, width), F32),
            pltpu.VMEM((8, 128), F32),
            pltpu.VMEM((4, width), F32),
            dma((pieces,)),
            dma,
            dma((1 + chunks,)),
            dma((gvec_size, chunks)),
            dma((gvec_size, chunks)),
            dma((gvec_size, chunks, pieces)),
            dma((gvec_size, chunks, pieces)),
            dma((3, total)),
            dma((3, total)),
        ],
        compiler_params=pltpu.CompilerParams(
            collective_id=0, has_side_effects=True, vmem_limit_bytes=58 * 1024 * 1024
        ),
        name="step",
    )(
        near_list, live_count, atom_pos, atom_charge.reshape(1, atoms), jnp.asarray(pair),
        jnp.asarray(diagonal), jnp.asarray(groups), jnp.asarray(bands), coeffs, v_local,
    )
    return (waves_new, misc[0, :1], misc[1, :1], atom_force, misc[2, :8])


def solution(mesh):
    sizes = (mesh.shape["band"], mesh.shape["gvec"], mesh.shape["dom"])
    return jax.shard_map(
        functools.partial(per_device, sizes),
        mesh=mesh,
        in_specs=(
            P(("band", "dom"), "gvec", None, None),
            P(None, "gvec", None),
            P(None, ("band", "gvec", "dom")),
            P(("band", "gvec", "dom")),
            P(("band", "gvec", "dom")),
            P(("band", "gvec", "dom")),
        ),
        out_specs=(
            P(("band", "dom"), "gvec", None, None),
            P(("band", "dom")),
            P(("band", "dom")),
            P(None, ("band", "gvec", "dom")),
            P(),
        ),
        check_vma=False,
    )
```

time: 112 us -> 81.2 us (0.72)
  Pallas kernels: 47.5 us -> 73.4 us
  matrix products: 23 us -> 0 us
  other arithmetic: 18.6 us -> 0 us
  waiting for transfers between devices: 6.7 us -> 0 us
  starting transfers between devices: 4.11 us -> 0 us
  local copies, waits for them, and re-layouts: 8.13 us -> 6.25 us
  between operations: 3.05 us -> 1.29 us
    pallas_call x5 -> x1, Pallas kernels: 47.5 us -> 73.4 us  [per_device(): pl.pallas_call(functools.partial(step_kernel, sizes, plan), out_shape=(ja...]
    dot_general x20 -> x0, matrix products: 23 us -> none  [the longest x4 9.74 us: per_device(): jnp.einsum('nayz,yq->naqz', block, y_rows(step, part), preferred_element_...]
    ppermute x4 -> x0, waiting for transfers between devices: 6.7 us -> none  [shift(): lax.ppermute(value, 'gvec', [(at, (at + step) % gvec_size) for at in rang...]
    convert_element_type x6 -> x0, other arithmetic: 6.55 us -> none  [the longest x1 6.38 us: per_device(): (field_total[None, :, window] * real_space.astype(jnp.float32)).astype(jn...]
    concatenate x6 -> x0, other arithmetic: 5.23 us -> none  [the longest x4 4.04 us: kernels(): return (jnp.concatenate(values, axis=1), jnp.concatenate(slopes, axis=1))]
    ppermute x4 -> x0, starting transfers between devices: 4.11 us -> none  [shift(): lax.ppermute(value, 'gvec', [(at, (at + step) % gvec_size) for at in rang...]
    reduce_sum x7 -> x0, other arithmetic: 2.19 us -> none  [the longest x1 0.72 us: per_device(): jnp.sum(moments[1] * z_value, axis=0)]
    mul x6 -> x0, other arithmetic: 2.13 us -> none  [the longest x2 1.39 us: kernels(): slopes.append(2.0 * exponent * offset * gauss_value)]
  transfers between devices with their start and end apart: 4 -> 0, of which waited for: 1 -> 0; matrix products, arithmetic and copies ran while one was open for 16% -> 0% of each run, Pallas kernels for 20% -> 0%
where the time goes in v1:
time: 81.2 us; the launch traced here: 80.9 us
  Pallas kernels  73.4 us (90%)
  local copies, waits for them, and re-layouts  6.25 us (8%)
  between operations  1.29 us (2%)
    pallas_call x1, Pallas kernels, per_device(): pl.pallas_call(functools.partial(step_kernel, sizes, plan), out_shape=(ja...  73.4 us
    unnamed x4, local copies, waits for them, and re-layouts  3.78 us

profile of v1, /device:TPU:0, one launch (start us, length us, event | category | flops | bytes accessed | tf_op | source)
XLA Modules:
  0.0 80.9 jit_solution(7711823940906851876)
XLA Ops:
  1.3 73.4 %step.1 = (bf16[1,64,128,128]{3,2,1,0:T(8,128)(2,1)}, f32[3,1024]{1,0:T(4,128)}, f32[8,128]{1,0:T(8,128)}) custom-call(s32[16]{0:T(128)} %near_ref.1, s32[1]{0:T(128)S(6)} %copy.17.live_ref, f32[3,1024]{1,0:T(4,128)} %pos_ref.1, f32[1,1024]{1,0:T(1,128)} %bitcast.5, bf16[2,128,128]{2,1,0:T(8,128)(2,1)} %constant.8.clone.cos_ref, ...), custom_call_target="tpu_custom_call" | custom-call | tf_op jit(solution)/shard_map/step/pallas_call | solution.py:572
  74.6 1.3 %fusion = (f32[1,1]{1,0:T(1,128)}, f32[1,1]{1,0:T(1,128)}) fusion(f32[8,128]{1,0:T(8,128)} %get-tuple-element.9), kind=kLoop, calls=%fused_computation.1 | loop fusion | bytes 16 | tf_op jit(solution)/shard_map/slice | solution.py:628
  75.9 1.2 %slice_bitcast_fusion = f32[8]{0:T(128)} fusion(f32[8,128]{1,0:T(8,128)} %get-tuple-element.9), kind=kLoop, calls=%fused_computation | loop fusion | bytes 64 | tf_op jit(solution)/shard_map/squeeze | solution.py:628
  77.1 0.0 copy-start
  77.1 3.2 %copy.18 = bf16[1,64,128,128]{3,2,1,0:T(8,128)(2,1)} copy(bf16[1,64,128,128]{3,2,1,0:T(8,128)(2,1)} %get-tuple-element.18) | data formatting | bytes 4194304
  80.3 0.0 copy-done
  80.3 0.6 copy.19
Async XLA Ops:
  77.1 3.2 %copy-start = (f32[3,1024]{1,0:T(4,128)S(1)}, f32[3,1024]{1,0:T(4,128)}, u32[]{:S(2)}) copy-start(f32[3,1024]{1,0:T(4,128)} %get-tuple-element.21) | copy-start | bytes 36868

commit v2 on v1

--- a/solution.py
+++ b/solution.py
@@ -59,12 +59,12 @@
 
 def step_kernel(
     sizes, plan,
-    near_ref, live_ref, pos_ref, charge_ref, cos_ref, diag_ref, group_ref, band_ref, coeff_hbm, local_hbm,
+    near_hbm, live_ref, pos_hbm, charge_hbm, cos_hbm, diag_hbm, group_hbm, band_hbm, coeff_hbm, local_hbm,
     waves_ref, force_out, misc_ref,
-    coeff_ref, local_ref, stage_ref, sect_ref, held_ref, field_ref, dens_ref, going_ref, back_ref,
+    near_ref, pos_ref, charge_ref, cos_ref, diag_ref, group_ref, band_ref, coeff_ref, local_ref, stage_ref, sect_ref, held_ref, field_ref, dens_ref, going_ref, back_ref,
     image_ref, recip_ref, moment_ref, row_ref, rows_ref, tile_ref, tiles_ref, last_ref, lasts_ref,
     xg_ref, xh_ref, yg_ref, y_ref, depth_ref, zg_ref, zh_ref, scale_ref, place_ref, proj_ref,
-    load_sem, local_sem, own_sem, fsend, frecv, bsend, brecv, csend, crecv,
+    load_sem, local_sem, small_sem, own_sem, fsend, frecv, bsend, brecv, csend, crecv,
 ):
     band_size, gvec_size, dom_size = sizes
     total = band_size * gvec_size * dom_size
@@ -81,28 +81,36 @@
     pieces = x_local // piece
     barrier = pltpu.get_barrier_semaphore()
 
-    def peer_of(step):
-        outer = step // gvec_size
-        return (
-            lax.rem(band_id + outer // dom_size, band_size),
-            lax.rem(gvec_id + step % gvec_size, gvec_size),
-            lax.rem(dom_id + outer % dom_size, dom_size),
-        )
-
-    def greet(step, carry):
-        pl.semaphore_signal(barrier, inc=1, device_id=peer_of(step), device_id_type=MESH)
-        return carry
-
-    lax.fori_loop(1, total, greet, 0)
-
     def load_of(part):
         window = pl.ds(part * piece, piece)
         return pltpu.make_async_copy(coeff_hbm.at[0, window], coeff_ref.at[window], load_sem.at[part])
 
+    smalls = [
+        pltpu.make_async_copy(source, target, small_sem.at[at])
+        for at, (source, target) in enumerate(
+            (
+                (near_hbm, near_ref), (pos_hbm, pos_ref), (charge_hbm, charge_ref),
+                (cos_hbm, cos_ref), (diag_hbm, diag_ref), (group_hbm, group_ref), (band_hbm, band_ref),
+            )
+        )
+    ]
+    for copy in smalls:
+        copy.start()
     for part in range(pieces):
         load_of(part).start()
     local_copy = pltpu.make_async_copy(local_hbm, local_ref, local_sem)
     local_copy.start()
+
+    band_at = [lax.rem(band_id + shift, band_size) for shift in range(band_size)]
+    gvec_at = [lax.rem(gvec_id + shift, gvec_size) for shift in range(gvec_size)]
+    dom_at = [lax.rem(dom_id + shift, dom_size) for shift in range(dom_size)]
+
+    def peer_of(step):
+        outer = step // gvec_size
+        return band_at[outer // dom_size], gvec_at[step % gvec_size], dom_at[outer % dom_size]
+
+    for step in range(1, total):
+        pl.semaphore_signal(barrier, inc=1, device_id=peer_of(step), device_id_type=MESH)
 
     def broadcast(kind, src, dst):
         def copy_of(step):
@@ -112,21 +120,18 @@
                 device_id=peer_of(step), device_id_type=MESH,
             )
 
-        def send(step, carry):
-            copy_of(step).start()
-            return carry
-
-        def finish(step, carry):
-            copy_of(step).wait()
-            return carry
-
         def start():
-            lax.fori_loop(1, total, send, 0)
+            for step in range(1, total):
+                copy_of(step).start()
 
         def wait(first, stop):
-            lax.fori_loop(first, stop, finish, 0)
+            for step in range(first, stop):
+                copy_of(step).wait()
 
         return start, wait
+
+    for copy in smalls:
+        copy.wait()
 
     lanes = row_ref.shape[1]
     lane = iota((1, lanes), 1)
@@ -170,24 +175,39 @@
         lax.fori_loop(0, extent // 8, spread, 0)
         return carry
 
-    lax.fori_loop(0, pieces, forward, 0)
-    pl.semaphore_wait(barrier, total - 1)
-
-    start_rows, wait_rows = broadcast(0, row_ref, rows_ref)
-    start_rows()
+    ahead = pieces // 2
 
     def gvec_peer(step):
-        return (band_id, lax.rem(gvec_id + step, gvec_size), dom_id)
+        return (band_id, gvec_at[step], dom_id)
+
+    def lead_copy(step):
+        owner = gvec_at[step]
+        window = pl.ds(0, ahead * piece)
+        return pltpu.make_async_remote_copy(
+            src_ref=sect_ref.at[pl.ds(owner * y_share, y_share), window],
+            dst_ref=held_ref.at[gvec_id, :, window],
+            send_sem=fsend.at[step, chunks], recv_sem=frecv.at[step, chunks],
+            device_id=gvec_peer(step), device_id_type=MESH,
+        )
 
     def forward_copy(step, chunk):
-        owner = lax.rem(gvec_id + step, gvec_size)
+        owner = gvec_at[step]
+        window = pl.ds(ahead * piece, x_local - ahead * piece)
         return pltpu.make_async_remote_copy(
-            src_ref=sect_ref.at[pl.ds(owner * y_share + chunk * y_chunk, y_chunk)],
-            dst_ref=held_ref.at[gvec_id, pl.ds(chunk * y_chunk, y_chunk)],
+            src_ref=sect_ref.at[pl.ds(owner * y_share + chunk * y_chunk, y_chunk), window],
+            dst_ref=held_ref.at[gvec_id, pl.ds(chunk * y_chunk, y_chunk), window],
             send_sem=fsend.at[step, chunk], recv_sem=frecv.at[step, chunk],
             device_id=gvec_peer(step), device_id_type=MESH,
         )
 
+    start_rows, wait_rows = broadcast(0, row_ref, rows_ref)
+    lax.fori_loop(0, ahead, forward, 0)
+    pl.semaphore_wait(barrier, total - 1)
+    start_rows()
+    if ahead:
+        for step in range(1, gvec_size):
+            lead_copy(step).start()
+    lax.fori_loop(ahead, pieces, forward, 0)
     for chunk in range(chunks):
         for step in range(1, gvec_size):
             forward_copy(step, chunk).start()
@@ -255,28 +275,36 @@
             y_ref[1, k * live_total // 128 + part] = slope[:, part * 128 : (part + 1) * 128]
         away = x_points - centre[2]
         value = jnp.exp(-exponent * away * away)
-        depth_ref[:, window] = (scaled * value).astype(BF16)
+        depth_ref[window] = jnp.transpose(scaled * value).astype(BF16)
         zg_ref[:, window] = value.astype(BF16)
         zh_ref[:, window] = (2.0 * exponent * away * value).astype(BF16)
 
     block = min(width, 512)
 
-    def add_field(y, carry):
+    field_rows = 4
+
+    def add_field(index, carry):
         value = None
         for part in range(width // block):
             window = slice(part * block, (part + 1) * block)
-            plane = (xg_ref[:, window] * yg_ref[pl.ds(y, 1), window]).astype(BF16)
-            term = lax.dot_general(
-                plane, depth_ref[:, window], (((1,), (1,)), ((), ())), preferred_element_type=F32
+            plane = jnp.concatenate(
+                [
+                    (xg_ref[:, window] * yg_ref[pl.ds(index * field_rows + side, 1), window]).astype(BF16)
+                    for side in range(field_rows)
+                ],
+                axis=0,
             )
+            term = dot(plane, depth_ref[window])
             value = term if value is None else value + term
-        field_ref[y] += value.astype(BF16).astype(F32)
+        value = value.astype(BF16).astype(F32)
+        for side in range(field_rows):
+            field_ref[index * field_rows + side] += value[side * extent : (side + 1) * extent]
         return carry
 
-    lax.fori_loop(0, y_share, add_field, 0)
+    lax.fori_loop(0, y_share // field_rows, add_field, 0)
 
     def back_copy(step, chunk, part):
-        owner = lax.rem(gvec_id + step, gvec_size)
+        owner = gvec_at[step]
         return pltpu.make_async_remote_copy(
             src_ref=going_ref.at[chunk, pl.ds(owner * x_local + part * piece, piece)],
             dst_ref=back_ref.at[gvec_id, chunk, pl.ds(part * piece, piece)],
@@ -291,6 +319,10 @@
         )
 
     own_copy.wait()
+
+    if ahead:
+        for step in range(1, gvec_size):
+            lead_copy(step).wait_recv()
 
     def middle(chunk, carry):
         for step in range(1, gvec_size):
@@ -365,36 +397,33 @@
     )
     stress = [weight * total_of(term) / cells for term in terms]
 
-    y_block = 16 if y_share % 16 == 0 else y_share
     x_part = 32
 
     def project(index, carry):
         at = pl.ds(pl.multiple_of(index * 128, 128), 128)
         tables = jnp.concatenate([zg_ref[:, at], zh_ref[:, at]], axis=1)
-        sums = [jnp.zeros((1, 128), F32) for _ in range(4)]
-        for x_at in range(extent // x_part):
-            x_window = pl.ds(x_at * x_part, x_part)
-
-            def over_y(outer, accs):
-                along, slope, deep = accs
-                left = dens_ref[pl.ds(outer * y_block, y_block), x_window].reshape(y_block * x_part, extent)
-                result = dot(left, tables)
-                for inner in range(y_block):
-                    y = outer * y_block + inner
-                    rows_at = slice(inner * x_part, (inner + 1) * x_part)
-                    value, derivative = y_ref[0, index, pl.ds(y, 1)], y_ref[1, index, pl.ds(y, 1)]
-                    along = along + result[rows_at, :128] * value
-                    slope = slope + result[rows_at, :128] * derivative
-                    deep = deep + result[rows_at, 128:] * value
-                return along, slope, deep
-
-            start = tuple(jnp.zeros((x_part, 128), F32) for _ in range(3))
-            along, slope, deep = lax.fori_loop(0, y_share // y_block, over_y, start)
+
+        def over_x(x_at, sums):
+            x_window = pl.ds(pl.multiple_of(x_at * x_part, x_part), x_part)
+            result = dot(dens_ref[:, x_window].reshape(y_share * x_part, extent), tables)
+            along, slope, deep = 0.0, 0.0, 0.0
+            for y in range(y_share):
+                rows_at = slice(y * x_part, (y + 1) * x_part)
+                value, derivative = y_ref[0, index, pl.ds(y, 1)], y_ref[1, index, pl.ds(y, 1)]
+                along = along + result[rows_at, :128] * value
+                slope = slope + result[rows_at, :128] * derivative
+                deep = deep + result[rows_at, 128:] * value
             value, derivative = xg_ref[x_window, at], xh_ref[x_window, at]
-            for at_sum, term in enumerate((derivative * along, value * slope, value * deep, value * along)):
-                sums[at_sum] = sums[at_sum] + jnp.sum(term, axis=0, keepdims=True)
+            terms = (derivative * along, value * slope, value * deep, value * along)
+            return tuple(
+                old + jnp.sum(term.reshape(-1, 8, 128), axis=0) for old, term in zip(sums, terms)
+            )
+
+        start = tuple(jnp.zeros((8, 128), F32) for _ in range(4))
+        sums = lax.fori_loop(0, extent // x_part, over_x, start)
         for at_sum in range(4):
-            proj_ref[at_sum : at_sum + 1, at] = sums[at_sum] * scale_ref[:, at]
+            total_row = jnp.sum(sums[at_sum], axis=0, keepdims=True)
+            proj_ref[at_sum : at_sum + 1, at] = total_row * scale_ref[:, at]
         return carry
 
     lax.fori_loop(0, width // 128, project, 0)
@@ -415,7 +444,28 @@
     for chunk in range(chunks):
         own_back(chunk).wait()
     norms, inners, squares = [], [], []
+
+    def force_to_atoms():
+        wait_tiles(1, total)
+        summed = tiles_ref[0]
+        for source in range(1, total):
+            summed = summed + tiles_ref[source]
+        slot_lanes = (iota((live_total, 128), 0).astype(F32) - place_ref[0:1, 0:1]) == iota(
+            (live_total, 128), 1
+        ).astype(F32)
+        slot_lanes = slot_lanes & (iota((live_total, 128), 1) < live)
+        slot_force = jnp.dot(summed, slot_lanes.astype(F32), precision=HIGH, preferred_element_type=F32)
+        near_column = jnp.full((128, 1), -1, jnp.int32)
+        for slot in range(cap):
+            near_column = jnp.where(iota((128, 1), 0) == slot, near_ref[slot], near_column)
+        at_atom = (iota((128, atoms), 1) == near_column).astype(F32)
+        atom_force = jnp.dot(slot_force, at_atom, precision=HIGH, preferred_element_type=F32)
+        force_out[...] = atom_force[0:3]
+        return summed
+
     for part in range(pieces):
+        if part == pieces - 1:
+            summed = force_to_atoms()
         for chunk in range(chunks):
             for step in range(1, gvec_size):
                 back_copy(step, chunk, part).wait_recv()
@@ -511,22 +561,6 @@
 
     lax.fori_loop(0, x_local // 4, update, 0)
 
-    wait_tiles(1, total)
-    summed = tiles_ref[0]
-    for source in range(1, total):
-        summed = summed + tiles_ref[source]
-    slot_lanes = (iota((live_total, 128), 0).astype(F32) - place_ref[0:1, 0:1]) == iota(
-        (live_total, 128), 1
-    ).astype(F32)
-    slot_lanes = slot_lanes & (iota((live_total, 128), 1) < live)
-    slot_force = jnp.dot(summed, slot_lanes.astype(F32), precision=HIGH, preferred_element_type=F32)
-    near_column = jnp.full((128, 1), -1, jnp.int32)
-    for slot in range(cap):
-        near_column = jnp.where(iota((128, 1), 0) == slot, near_ref[slot], near_column)
-    at_atom = (iota((128, atoms), 1) == near_column).astype(F32)
-    atom_force = jnp.dot(slot_force, at_atom, precision=HIGH, preferred_element_type=F32)
-    force_out[...] = atom_force[0:3]
-
     wait_last(gvec_size, total)
     lasts = lasts_ref[:, 0, :]
     both = jnp.dot(group_ref[0], lasts, precision=HIGH, preferred_element_type=F32)
@@ -540,6 +574,8 @@
     misc_ref[3:8] = jnp.zeros((5, 128), F32)
 
     for step in range(1, gvec_size):
+        if ahead:
+            lead_copy(step).wait_send()
         for chunk in range(chunks):
             forward_copy(step, chunk).wait_send()
             for part in range(pieces):
@@ -565,10 +601,17 @@
     groups, bands = group_tables(sizes)
     vmem = pl.BlockSpec(memory_space=pltpu.VMEM)
     smem = pl.BlockSpec(memory_space=pltpu.SMEM)
-    hbm = pl.BlockSpec(memory_space=pl.ANY)
+    hbm = pl.BlockSpec(memory_space=pltpu.HBM)
     plan = (x_local, extent, y_share, cap, live_total, atoms)
     deep = max(piece, y_chunk, 16)
     dma = pltpu.SemaphoreType.DMA
+    operands = [
+        pltpu.with_memory_space_constraint(operand, pltpu.HBM)
+        for operand in (
+            near_list, atom_pos, atom_charge.reshape(1, atoms), jnp.asarray(pair),
+            jnp.asarray(diagonal), jnp.asarray(groups), jnp.asarray(bands), coeffs, v_local,
+        )
+    ]
     waves_new, atom_force, misc = pl.pallas_call(
         functools.partial(step_kernel, sizes, plan),
         out_shape=(
@@ -576,9 +619,16 @@
             jax.ShapeDtypeStruct((3, atoms), F32),
             jax.ShapeDtypeStruct((8, 128), F32),
         ),
-        in_specs=[smem, smem, vmem, vmem, vmem, vmem, vmem, vmem, hbm, hbm],
+        in_specs=[hbm, smem] + [hbm] * 8,
         out_specs=(vmem, vmem, vmem),
         scratch_shapes=[
+            pltpu.SMEM(near_list.shape, jnp.int32),
+            pltpu.VMEM(atom_pos.shape, F32),
+            pltpu.VMEM((1, atoms), F32),
+            pltpu.VMEM(pair.shape, BF16),
+            pltpu.VMEM(diagonal.shape, BF16),
+            pltpu.VMEM(groups.shape, F32),
+            pltpu.VMEM(bands.shape, F32),
             pltpu.VMEM((x_local, extent, extent), BF16),
             pltpu.VMEM(v_local.shape, BF16),
             pltpu.VMEM((deep * extent, extent), F32),
@@ -601,7 +651,7 @@
             pltpu.VMEM((extent, width), F32),
             pltpu.VMEM((y_share, width), F32),
             pltpu.VMEM((2, width // 128, y_share, 128), F32),
-            pltpu.VMEM((extent, width), BF16),
+            pltpu.VMEM((width, extent), BF16),
             pltpu.VMEM((extent, width), BF16),
             pltpu.VMEM((extent, width), BF16),
             pltpu.VMEM((1, width), F32),
@@ -609,22 +659,20 @@
             pltpu.VMEM((4, width), F32),
             dma((pieces,)),
             dma,
+            dma((7,)),
             dma((1 + chunks,)),
-            dma((gvec_size, chunks)),
-            dma((gvec_size, chunks)),
+            dma((gvec_size, chunks + 1)),
+            dma((gvec_size, chunks + 1)),
             dma((gvec_size, chunks, pieces)),
             dma((gvec_size, chunks, pieces)),
             dma((3, total)),
             dma((3, total)),
         ],
         compiler_params=pltpu.CompilerParams(
-            collective_id=0, has_side_effects=True, vmem_limit_bytes=58 * 1024 * 1024
+            collective_id=0, has_side_effects=True, vmem_limit_bytes=36 * 1024 * 1024
         ),
         name="step",
-    )(
-        near_list, live_count, atom_pos, atom_charge.reshape(1, atoms), jnp.asarray(pair),
-        jnp.asarray(diagonal), jnp.asarray(groups), jnp.asarray(bands), coeffs, v_local,
-    )
+    )(operands[0], live_count, *operands[1:])
     return (waves_new, misc[0, :1], misc[1, :1], atom_force, misc[2, :8])
 
 

time: 81.2 us -> 72 us (0.89)
  Pallas kernels: 73.4 us -> 67.6 us
  local copies, waits for them, and re-layouts: 6.25 us -> 2.96 us
    pallas_call x1, Pallas kernels: 73.4 us -> 67.6 us  [per_device(): pl.pallas_call(functools.partial(step_kernel, sizes, plan), out_shape=(ja...]
    unnamed x4 -> x2, local copies, waits for them, and re-layouts: 3.78 us -> 1.92 us
where the time goes in v2:
time: 72 us; the launch traced here: 71.9 us
  Pallas kernels  67.6 us (94%)
  local copies, waits for them, and re-layouts  2.96 us (4%)
  between operations  1.29 us (2%)
    pallas_call x1, Pallas kernels, per_device(): pl.pallas_call(functools.partial(step_kernel, sizes, plan), out_shape=(ja...  67.6 us
    unnamed x2, local copies, waits for them, and re-layouts  1.92 us

profile of v2, /device:TPU:0, one launch (start us, length us, event | category | flops | bytes accessed | tf_op | source)
XLA Modules:
  0.0 71.9 jit_solution(7394079381508105371)
XLA Ops:
  1.3 67.6 %step.1 = (bf16[1,64,128,128]{3,2,1,0:T(8,128)(2,1)S(1)}, f32[3,1024]{1,0:T(4,128)S(1)}, f32[8,128]{1,0:T(8,128)S(1)}) custom-call(s32[16]{0:T(128)} %near_hbm.1, s32[1]{0:T(128)S(6)} %copy.17.live_ref, f32[3,1024]{1,0:T(4,128)} %pos_hbm.1, f32[1,1024]{1,0:T(1,128)} %bitcast.5, bf16[2,128,128]{2,1,0:T(8,128)(2,1)} %constant.8.clone.cos_hbm, ...), custom_call_target="tpu_custom_call" | custom-call | tf_op jit(solution)/shard_map/step/pallas_call | solution.py:615
  68.9 0.5 fusion
  69.5 0.5 slice_bitcast_fusion
  70.0 1.3 %copy.18 = bf16[1,64,128,128]{3,2,1,0:T(8,128)(2,1)} copy(bf16[1,64,128,128]{3,2,1,0:T(8,128)(2,1)S(1)} %get-tuple-element.18) | data formatting | bytes 4194304
  71.3 0.6 copy.19

commit v3 on v2

--- a/solution.py
+++ b/solution.py
@@ -35,16 +35,6 @@
     return pair, diagonal
 
 
-def group_tables(sizes):
-    band_size, gvec_size, dom_size = sizes
-    total = band_size * gvec_size * dom_size
-    at = np.arange(total)
-    group = (at // (gvec_size * dom_size)) * dom_size + at % dom_size
-    same = (group[:, None] == group[None, :]).astype(np.float32)
-    before = (at[None, :] < at[:, None]).astype(np.float32)
-    return np.stack([same, before]), group.astype(np.float32)[:, None]
-
-
 def dot(left, right):
     return jnp.dot(left, right, preferred_element_type=F32)
 
@@ -59,9 +49,9 @@
 
 def step_kernel(
     sizes, plan,
-    near_hbm, live_ref, pos_hbm, charge_hbm, cos_hbm, diag_hbm, group_hbm, band_hbm, coeff_hbm, local_hbm,
+    near_hbm, live_ref, pos_hbm, charge_hbm, cos_hbm, diag_hbm, group_hbm, coeff_hbm, local_hbm,
     waves_ref, force_out, misc_ref,
-    near_ref, pos_ref, charge_ref, cos_ref, diag_ref, group_ref, band_ref, coeff_ref, local_ref, stage_ref, sect_ref, held_ref, field_ref, dens_ref, going_ref, back_ref,
+    near_ref, pos_ref, charge_ref, cos_ref, diag_ref, group_ref, coeff_ref, local_ref, stage_ref, sect_ref, held_ref, field_ref, dens_ref, going_ref, back_ref,
     image_ref, recip_ref, moment_ref, row_ref, rows_ref, tile_ref, tiles_ref, last_ref, lasts_ref,
     xg_ref, xh_ref, yg_ref, y_ref, depth_ref, zg_ref, zh_ref, scale_ref, place_ref, proj_ref,
     load_sem, local_sem, small_sem, own_sem, fsend, frecv, bsend, brecv, csend, crecv,
@@ -79,6 +69,9 @@
     chunks = y_share // y_chunk
     piece = 16 if x_local % 16 == 0 else x_local
     pieces = x_local // piece
+    grain = 8 if x_local % 8 == 0 else x_local
+    grains = x_local // grain
+    early = max(chunks - 2, 0)
     barrier = pltpu.get_barrier_semaphore()
 
     def load_of(part):
@@ -90,7 +83,7 @@
         for at, (source, target) in enumerate(
             (
                 (near_hbm, near_ref), (pos_hbm, pos_ref), (charge_hbm, charge_ref),
-                (cos_hbm, cos_ref), (diag_hbm, diag_ref), (group_hbm, group_ref), (band_hbm, band_ref),
+                (cos_hbm, cos_ref), (diag_hbm, diag_ref), (group_hbm, group_ref),
             )
         )
     ]
@@ -130,8 +123,63 @@
 
         return start, wait
 
-    for copy in smalls:
-        copy.wait()
+    group = piece
+    smalls[3].wait()
+    smalls[4].wait()
+
+    def forward(index, carry):
+        load_of(index).wait()
+        for pair in range(group // 2):
+            first = index * group + 2 * pair
+            both = jnp.concatenate([coeff_ref[first], coeff_ref[first + 1]], axis=1)
+            section = dot(both, diag_ref[0]).astype(BF16)
+            result = dot(cos_ref[0], section)
+            stage_ref[pl.ds(2 * pair * extent, extent)] = result[:, :extent]
+            stage_ref[pl.ds((2 * pair + 1) * extent, extent)] = result[:, extent:]
+        window = pl.ds(pl.multiple_of(index * group, group), group)
+
+        def spread(outer, inner_carry):
+            for inner in range(8):
+                y = outer * 8 + inner
+                sect_ref[y, window] = stage_ref[pl.ds(y, group, stride=extent)].astype(BF16)
+            return inner_carry
+
+        lax.fori_loop(0, extent // 8, spread, 0)
+        return carry
+
+    ahead = pieces // 2
+
+    def gvec_peer(step):
+        return (band_id, gvec_at[step], dom_id)
+
+    def lead_copy(step, part):
+        window = pl.ds(part * piece, piece)
+        return pltpu.make_async_remote_copy(
+            src_ref=sect_ref.at[pl.ds(gvec_at[step] * y_share, y_share), window],
+            dst_ref=held_ref.at[gvec_id, :, window],
+            send_sem=fsend.at[step, chunks + part], recv_sem=frecv.at[step, chunks + part],
+            device_id=gvec_peer(step), device_id_type=MESH,
+        )
+
+    def forward_copy(step, chunk):
+        owner = gvec_at[step]
+        window = pl.ds(ahead * piece, x_local - ahead * piece)
+        return pltpu.make_async_remote_copy(
+            src_ref=sect_ref.at[pl.ds(owner * y_share + chunk * y_chunk, y_chunk), window],
+            dst_ref=held_ref.at[gvec_id, pl.ds(chunk * y_chunk, y_chunk), window],
+            send_sem=fsend.at[step, chunk], recv_sem=frecv.at[step, chunk],
+            device_id=gvec_peer(step), device_id_type=MESH,
+        )
+
+    if ahead:
+        forward(0, 0)
+    pl.semaphore_wait(barrier, total - 1)
+    if ahead:
+        for step in range(1, gvec_size):
+            lead_copy(step, 0).start()
+
+    for at in (0, 1, 2, 5):
+        smalls[at].wait()
 
     lanes = row_ref.shape[1]
     lane = iota((1, lanes), 1)
@@ -152,61 +200,16 @@
     row = jnp.where(lane == 4 * cap, live.astype(F32), row)
     row_ref[...] = row
     rows_ref[me] = row
-
-    group = piece
-
-    def forward(index, carry):
-        load_of(index).wait()
-        for pair in range(group // 2):
-            first = index * group + 2 * pair
-            both = jnp.concatenate([coeff_ref[first], coeff_ref[first + 1]], axis=1)
-            section = dot(both, diag_ref[0]).astype(BF16)
-            result = dot(cos_ref[0], section)
-            stage_ref[pl.ds(2 * pair * extent, extent)] = result[:, :extent]
-            stage_ref[pl.ds((2 * pair + 1) * extent, extent)] = result[:, extent:]
-        window = pl.ds(pl.multiple_of(index * group, group), group)
-
-        def spread(outer, inner_carry):
-            for inner in range(8):
-                y = outer * 8 + inner
-                sect_ref[y, window] = stage_ref[pl.ds(y, group, stride=extent)].astype(BF16)
-            return inner_carry
-
-        lax.fori_loop(0, extent // 8, spread, 0)
-        return carry
-
-    ahead = pieces // 2
-
-    def gvec_peer(step):
-        return (band_id, gvec_at[step], dom_id)
-
-    def lead_copy(step):
-        owner = gvec_at[step]
-        window = pl.ds(0, ahead * piece)
-        return pltpu.make_async_remote_copy(
-            src_ref=sect_ref.at[pl.ds(owner * y_share, y_share), window],
-            dst_ref=held_ref.at[gvec_id, :, window],
-            send_sem=fsend.at[step, chunks], recv_sem=frecv.at[step, chunks],
-            device_id=gvec_peer(step), device_id_type=MESH,
-        )
-
-    def forward_copy(step, chunk):
-        owner = gvec_at[step]
-        window = pl.ds(ahead * piece, x_local - ahead * piece)
-        return pltpu.make_async_remote_copy(
-            src_ref=sect_ref.at[pl.ds(owner * y_share + chunk * y_chunk, y_chunk), window],
-            dst_ref=held_ref.at[gvec_id, pl.ds(chunk * y_chunk, y_chunk), window],
-            send_sem=fsend.at[step, chunk], recv_sem=frecv.at[step, chunk],
-            device_id=gvec_peer(step), device_id_type=MESH,
-        )
-
     start_rows, wait_rows = broadcast(0, row_ref, rows_ref)
-    lax.fori_loop(0, ahead, forward, 0)
-    pl.semaphore_wait(barrier, total - 1)
     start_rows()
-    if ahead:
+
+    def lead(part, carry):
+        forward(part, carry)
         for step in range(1, gvec_size):
-            lead_copy(step).start()
+            lead_copy(step, part).start()
+        return carry
+
+    lax.fori_loop(1, ahead, lead, 0)
     lax.fori_loop(ahead, pieces, forward, 0)
     for chunk in range(chunks):
         for step in range(1, gvec_size):
@@ -240,7 +243,7 @@
     rows = rows_ref[:, 0, :]
     count = rows[:, 4 * cap : 4 * cap + 1]
     count_wide = jnp.broadcast_to(count, (total, live_total))
-    offset = jnp.dot(group_ref[1], count_wide, precision=HIGH, preferred_element_type=F32)
+    offset = jnp.dot(group_ref[...], count_wide, precision=HIGH, preferred_element_type=F32)
     order = iota((total, live_total), 1).astype(F32)
     holds = ((order >= offset) & (order < offset + count_wide)).astype(F32)
     slot_at = jnp.sum(holds * (order - offset), axis=0, keepdims=True)
@@ -306,8 +309,8 @@
     def back_copy(step, chunk, part):
         owner = gvec_at[step]
         return pltpu.make_async_remote_copy(
-            src_ref=going_ref.at[chunk, pl.ds(owner * x_local + part * piece, piece)],
-            dst_ref=back_ref.at[gvec_id, chunk, pl.ds(part * piece, piece)],
+            src_ref=going_ref.at[chunk, pl.ds(owner * x_local + part * grain, grain)],
+            dst_ref=back_ref.at[gvec_id, chunk, pl.ds(part * grain, grain)],
             send_sem=bsend.at[step, chunk, part], recv_sem=brecv.at[step, chunk, part],
             device_id=gvec_peer(step), device_id_type=MESH,
         )
@@ -320,9 +323,9 @@
 
     own_copy.wait()
 
-    if ahead:
-        for step in range(1, gvec_size):
-            lead_copy(step).wait_recv()
+    for step in range(1, gvec_size):
+        for part in range(ahead):
+            lead_copy(step, part).wait_recv()
 
     def middle(chunk, carry):
         for step in range(1, gvec_size):
@@ -352,13 +355,26 @@
             return inner_carry
 
         lax.fori_loop(0, extent // 8, spread, 0)
-        for part in range(pieces):
+        own_back(chunk).start()
+        return carry
+
+    def middle_early(chunk, carry):
+        middle(chunk, carry)
+        for part in range(grains):
             for step in range(1, gvec_size):
                 back_copy(step, chunk, part).start()
-        own_back(chunk).start()
-        return carry
-
-    lax.fori_loop(0, chunks, middle, 0)
+        return carry
+
+    lax.fori_loop(0, early, middle_early, 0)
+    lax.fori_loop(early, chunks, middle, 0)
+
+    def send_late(part, carry):
+        for chunk in range(early, chunks):
+            for step in range(1, gvec_size):
+                back_copy(step, chunk, part).start()
+        return carry
+
+    lax.fori_loop(0, grains, send_late, 0)
 
     q_wave = iota((extent, extent), 0).astype(F32) * wave_step
     l_wave = iota((extent, extent), 1).astype(F32) * wave_step
@@ -443,8 +459,6 @@
 
     for chunk in range(chunks):
         own_back(chunk).wait()
-    norms, inners, squares = [], [], []
-
     def force_to_atoms():
         wait_tiles(1, total)
         summed = tiles_ref[0]
@@ -463,65 +477,6 @@
         force_out[...] = atom_force[0:3]
         return summed
 
-    for part in range(pieces):
-        if part == pieces - 1:
-            summed = force_to_atoms()
-        for chunk in range(chunks):
-            for step in range(1, gvec_size):
-                back_copy(step, chunk, part).wait_recv()
-
-        def image_of(index, carry):
-            norm, inner = carry
-            for pair in range(2):
-                first = part * piece + 4 * index + 2 * pair
-                both = jnp.concatenate(
-                    [
-                        jnp.concatenate(
-                            [
-                                back_ref[source, chunk, first + side]
-                                for source in range(gvec_size)
-                                for chunk in range(chunks)
-                            ],
-                            axis=0,
-                        )
-                        for side in range(2)
-                    ],
-                    axis=1,
-                )
-                section = dot(cos_ref[1], both).astype(BF16)
-                waves = dot(section, diag_ref[1])
-                for side in range(2):
-                    a = first + side
-                    wide = coeff_ref[a].astype(F32)
-                    x_wave = x_wave_of(a)
-                    image = (0.5 * x_wave * x_wave + plane_kinetic) * wide
-                    image = image + waves[:, side * extent : (side + 1) * extent]
-                    image_ref[a] = image
-                    norm = norm + jnp.sum((wide * wide).reshape(-1, 8, extent), axis=0)
-                    inner = inner + jnp.sum((wide * image).reshape(-1, 8, extent), axis=0)
-            return norm, inner
-
-        empty = jnp.zeros((8, extent), F32)
-        norm, inner = lax.fori_loop(0, piece // 4, image_of, (empty, empty))
-        norm, inner = total_of(norm), total_of(inner)
-        filled = norm > 0.0
-        energy = jnp.where(filled, inner / jnp.where(filled, norm, 1.0), 0.0)
-
-        def residual_of(index, square):
-            for side in range(4):
-                a = part * piece + 4 * index + side
-                wide = coeff_ref[a].astype(F32)
-                image = image_ref[a]
-                residual = image - energy * wide
-                square = square + jnp.sum((residual * residual).reshape(-1, 8, extent), axis=0)
-                image_ref[a] = wide - image * recip_ref[a]
-            return square
-
-        square = total_of(lax.fori_loop(0, piece // 4, residual_of, empty))
-        norms.append(norm)
-        inners.append(inner)
-        squares.append(square)
-
     def merged(parts):
         norm = sum(part[0] for part in parts)
         inner = sum(part[1] for part in parts)
@@ -535,20 +490,66 @@
             square = square + part_square + away * away * part_norm
         return norm, inner, square
 
-    own = merged(list(zip(norms, inners, squares)))
-    last_lane = iota(last_ref.shape, 1)
-    last = jnp.zeros(last_ref.shape, F32)
+    def image_of(part, sums):
+        for chunk in range(chunks):
+            for step in range(1, gvec_size):
+                back_copy(step, chunk, part).wait_recv()
+        norm = jnp.zeros((8, extent), F32)
+        inner = jnp.zeros((8, extent), F32)
+        for pair in range(grain // 2):
+            first = part * grain + 2 * pair
+            both = jnp.concatenate(
+                [
+                    jnp.concatenate(
+                        [
+                            back_ref[source, chunk, first + side]
+                            for source in range(gvec_size)
+                            for chunk in range(chunks)
+                        ],
+                        axis=0,
+                    )
+                    for side in range(2)
+                ],
+                axis=1,
+            )
+            section = dot(cos_ref[1], both).astype(BF16)
+            waves = dot(section, diag_ref[1])
+            for side in range(2):
+                a = first + side
+                wide = coeff_ref[a].astype(F32)
+                x_wave = x_wave_of(a)
+                image = (0.5 * x_wave * x_wave + plane_kinetic) * wide
+                image = image + waves[:, side * extent : (side + 1) * extent]
+                image_ref[a] = image
+                norm = norm + jnp.sum((wide * wide).reshape(-1, 8, extent), axis=0)
+                inner = inner + jnp.sum((wide * image).reshape(-1, 8, extent), axis=0)
+        norm, inner = total_of(norm), total_of(inner)
+        filled = norm > 0.0
+        energy = jnp.where(filled, inner / jnp.where(filled, norm, 1.0), 0.0)
+        square = jnp.zeros((8, extent), F32)
+        for side in range(grain):
+            a = part * grain + side
+            wide = coeff_ref[a].astype(F32)
+            image = image_ref[a]
+            residual = image - energy * wide
+            square = square + jnp.sum((residual * residual).reshape(-1, 8, extent), axis=0)
+            image_ref[a] = wide - image * recip_ref[a]
+        return merged([sums, (norm, inner, total_of(square))])
+
+    nothing = jnp.zeros((1, 1), F32)
+    sums = lax.fori_loop(0, grains - 1, image_of, (nothing, nothing, nothing))
+    summed = force_to_atoms()
+    own = image_of(grains - 1, sums)
     for at, value in enumerate(own):
-        last = jnp.where(last_lane == at, value, last)
-    last_ref[...] = last
-    lasts_ref[me] = last
+        last_ref[at : at + 1] = jnp.broadcast_to(value, (1, 128))
+    lasts_ref[me] = last_ref[...]
     start_last, wait_last = broadcast(2, last_ref, lasts_ref)
     start_last()
     wait_last(1, gvec_size)
     parts = []
     for source in range(gvec_size):
         other = lasts_ref[(band_id * gvec_size + source) * dom_size + dom_id]
-        parts.append(tuple(other[:, at : at + 1] for at in range(3)))
+        parts.append(tuple(other[at : at + 1] for at in range(3)))
     norm, inner, square = merged(parts)
     energy = inner / norm
 
@@ -562,24 +563,46 @@
     lax.fori_loop(0, x_local // 4, update, 0)
 
     wait_last(gvec_size, total)
-    lasts = lasts_ref[:, 0, :]
-    both = jnp.dot(group_ref[0], lasts, precision=HIGH, preferred_element_type=F32)
-    band_energy = both[:, 1:2] / both[:, 0:1]
-    occupied = 2.0 / (1.0 + jnp.exp((band_ref[...] - 0.5 * band_total) / (0.125 * band_total)))
-    band_sum = jnp.sum(occupied * band_energy, axis=0, keepdims=True) / float(gvec_size * band_total)
+    band_sum = jnp.zeros((1, 128), F32)
+    for band in range(band_size):
+        for dom in range(dom_size):
+            both = 0.0
+            for source in range(gvec_size):
+                both = both + lasts_ref[(band * gvec_size + source) * dom_size + dom]
+            shifted = band * dom_size + dom - 0.5 * band_total
+            occupied = float(2.0 / (1.0 + np.exp(shifted / (0.125 * band_total))))
+            band_sum = band_sum + occupied * (both[1:2] / both[0:1])
     misc_lane = iota((1, 128), 1)
     misc_ref[0:1] = jnp.broadcast_to(energy, (1, 128))
     misc_ref[1:2] = jnp.broadcast_to(square / norm, (1, 128))
-    misc_ref[2:3] = jnp.where(misc_lane == 7, band_sum, summed[3:4, :128])
+    misc_ref[2:3] = jnp.where(misc_lane == 7, band_sum / float(band_total), summed[3:4, :128])
     misc_ref[3:8] = jnp.zeros((5, 128), F32)
 
     for step in range(1, gvec_size):
-        if ahead:
-            lead_copy(step).wait_send()
+        for part in range(ahead):
+            lead_copy(step, part).wait_send()
         for chunk in range(chunks):
             forward_copy(step, chunk).wait_send()
-            for part in range(pieces):
+            for part in range(grains):
                 back_copy(step, chunk, part).wait_send()
+
+
+def finish_kernel(parts, waves_ref, force_ref, misc_ref, waves_hbm, energy_ref, ratio_ref, force_out, total_ref, sems):
+    size = waves_ref.shape[1] // parts
+    copies = [
+        pltpu.make_async_copy(
+            waves_ref.at[:, pl.ds(part * size, size)], waves_hbm.at[:, pl.ds(part * size, size)], sems.at[part]
+        )
+        for part in range(parts)
+    ]
+    for copy in copies:
+        copy.start()
+    energy_ref[...] = misc_ref[0:1, 0:1]
+    ratio_ref[...] = misc_ref[1:2, 0:1]
+    total_ref[...] = misc_ref[2:3, 0:8]
+    force_out[...] = force_ref[...]
+    for copy in copies:
+        copy.wait()
 
 
 def per_device(sizes, coeffs, v_local, atom_pos, atom_charge, near_list, live_count):
@@ -596,9 +619,10 @@
     chunks = y_share // y_chunk
     piece = 16 if x_local % 16 == 0 else x_local
     pieces = x_local // piece
+    grains = x_local // (8 if x_local % 8 == 0 else x_local)
     lanes = -(-(4 * cap + 1) // 128) * 128
     pair, diagonal = constant_tables(extent)
-    groups, bands = group_tables(sizes)
+    groups = np.tril(np.ones((total, total), np.float32), -1)
     vmem = pl.BlockSpec(memory_space=pltpu.VMEM)
     smem = pl.BlockSpec(memory_space=pltpu.SMEM)
     hbm = pl.BlockSpec(memory_space=pltpu.HBM)
@@ -609,7 +633,7 @@
         pltpu.with_memory_space_constraint(operand, pltpu.HBM)
         for operand in (
             near_list, atom_pos, atom_charge.reshape(1, atoms), jnp.asarray(pair),
-            jnp.asarray(diagonal), jnp.asarray(groups), jnp.asarray(bands), coeffs, v_local,
+            jnp.asarray(diagonal), jnp.asarray(groups), coeffs, v_local,
         )
     ]
     waves_new, atom_force, misc = pl.pallas_call(
@@ -619,7 +643,7 @@
             jax.ShapeDtypeStruct((3, atoms), F32),
             jax.ShapeDtypeStruct((8, 128), F32),
         ),
-        in_specs=[hbm, smem] + [hbm] * 8,
+        in_specs=[hbm, smem] + [hbm] * 7,
         out_specs=(vmem, vmem, vmem),
         scratch_shapes=[
             pltpu.SMEM(near_list.shape, jnp.int32),
@@ -628,7 +652,6 @@
             pltpu.VMEM(pair.shape, BF16),
             pltpu.VMEM(diagonal.shape, BF16),
             pltpu.VMEM(groups.shape, F32),
-            pltpu.VMEM(bands.shape, F32),
             pltpu.VMEM((x_local, extent, extent), BF16),
             pltpu.VMEM(v_local.shape, BF16),
             pltpu.VMEM((deep * extent, extent), F32),
@@ -645,8 +668,8 @@
             pltpu.VMEM((total, 1, lanes), F32),
             pltpu.VMEM((4, live_total), F32),
             pltpu.VMEM((total, 4, live_total), F32),
-            pltpu.VMEM((1, 128), F32),
-            pltpu.VMEM((total, 1, 128), F32),
+            pltpu.VMEM((3, 128), F32),
+            pltpu.VMEM((total, 3, 128), F32),
             pltpu.VMEM((extent, width), F32),
             pltpu.VMEM((extent, width), F32),
             pltpu.VMEM((y_share, width), F32),
@@ -659,12 +682,12 @@
             pltpu.VMEM((4, width), F32),
             dma((pieces,)),
             dma,
-            dma((7,)),
+            dma((6,)),
             dma((1 + chunks,)),
-            dma((gvec_size, chunks + 1)),
-            dma((gvec_size, chunks + 1)),
-            dma((gvec_size, chunks, pieces)),
-            dma((gvec_size, chunks, pieces)),
+            dma((gvec_size, chunks + pieces // 2)),
+            dma((gvec_size, chunks + pieces // 2)),
+            dma((gvec_size, chunks, grains)),
+            dma((gvec_size, chunks, grains)),
             dma((3, total)),
             dma((3, total)),
         ],
@@ -673,7 +696,21 @@
         ),
         name="step",
     )(operands[0], live_count, *operands[1:])
-    return (waves_new, misc[0, :1], misc[1, :1], atom_force, misc[2, :8])
+    parts = 4 if x_local % 4 == 0 else 1
+    scalar = jax.ShapeDtypeStruct((1, 1), F32)
+    waves_new, energy, ratio, atom_force, totals = pl.pallas_call(
+        functools.partial(finish_kernel, parts),
+        out_shape=(
+            jax.ShapeDtypeStruct(coeffs.shape, BF16), scalar, scalar,
+            jax.ShapeDtypeStruct((3, atoms), F32), jax.ShapeDtypeStruct((1, 8), F32),
+        ),
+        in_specs=[vmem] * 3,
+        out_specs=(hbm, vmem, vmem, vmem, vmem),
+        scratch_shapes=[dma((parts,))],
+        compiler_params=pltpu.CompilerParams(vmem_limit_bytes=8 * 1024 * 1024),
+        name="finish",
+    )(waves_new, atom_force, misc)
+    return (waves_new, energy.reshape(1), ratio.reshape(1), atom_force, totals.reshape(8))
 
 
 def solution(mesh):

time: 72 us -> 66.5 us (0.924)
  local copies, waits for them, and re-layouts: 2.96 us -> 0 us
  Pallas kernels: 67.6 us -> 65.1 us
    pallas_call x1, Pallas kernels: 67.6 us -> 63.1 us  [per_device(): pl.pallas_call(functools.partial(step_kernel, sizes, plan), out_shape=(ja...]
    pallas_call x0 -> x1, Pallas kernels: none -> 1.96 us  [per_device(): pl.pallas_call(functools.partial(finish_kernel, parts), out_shape=(jax.Sh...]
    unnamed x2 -> x0, local copies, waits for them, and re-layouts: 1.92 us -> none
where the time goes in v3:
time: 66.5 us; the launch traced here: 66.4 us
  Pallas kernels  65.1 us (98%)
  between operations  1.29 us (2%)
    pallas_call x1, Pallas kernels, per_device(): pl.pallas_call(functools.partial(step_kernel, sizes, plan), out_shape=(ja...  63.1 us
    pallas_call x1, Pallas kernels, per_device(): pl.pallas_call(functools.partial(finish_kernel, parts), out_shape=(jax.Sh...  1.96 us

profile of v3, /device:TPU:0, one launch (start us, length us, event | category | flops | bytes accessed | tf_op | source)
XLA Modules:
  0.0 66.4 jit_solution(15210444972052523891)
XLA Ops:
  1.3 63.1 %step.1 = (bf16[1,64,128,128]{3,2,1,0:T(8,128)(2,1)S(1)}, f32[3,1024]{1,0:T(4,128)S(1)}, f32[8,128]{1,0:T(8,128)S(1)}) custom-call(s32[16]{0:T(128)} %near_hbm.1, s32[1]{0:T(128)S(6)} %copy.14.live_ref, f32[3,1024]{1,0:T(4,128)} %pos_hbm.1, f32[1,1024]{1,0:T(1,128)} %bitcast.4, bf16[2,128,128]{2,1,0:T(8,128)(2,1)} %constant.6.clone.cos_hbm, ...), custom_call_target="tpu_custom_call" | custom-call | tf_op jit(solution)/shard_map/step/pallas_call | solution.py:639
  64.4 2.0 %finish.1 = (bf16[1,64,128,128]{3,2,1,0:T(8,128)(2,1)}, f32[1,1]{1,0:T(1,128)}, f32[1,1]{1,0:T(1,128)}, f32[3,1024]{1,0:T(4,128)}, f32[1,8]{1,0:T(1,128)}) custom-call(bf16[1,64,128,128]{3,2,1,0:T(8,128)(2,1)S(1)} %get-tuple-element.13.waves_ref, f32[3,1024]{1,0:T(4,128)S(1)} %get-tuple-element.14.force_ref, f32[8,128]{1,0:T(8,128)S(1)} %get-tuple-element.15.misc_ref), custom_call_target="tpu_custom_call" | custom-call | tf_op jit(solution)/shard_map/finish/pallas_call | solution.py:701

commit v4 on v3

--- a/solution.py
+++ b/solution.py
@@ -51,8 +51,9 @@
     sizes, plan,
     near_hbm, live_ref, pos_hbm, charge_hbm, cos_hbm, diag_hbm, group_hbm, coeff_hbm, local_hbm,
     waves_ref, force_out, misc_ref,
-    near_ref, pos_ref, charge_ref, cos_ref, diag_ref, group_ref, coeff_ref, local_ref, stage_ref, sect_ref, held_ref, field_ref, dens_ref, going_ref, back_ref,
-    image_ref, recip_ref, moment_ref, row_ref, rows_ref, tile_ref, tiles_ref, last_ref, lasts_ref,
+    near_ref, pos_ref, charge_ref, cos_ref, diag_ref, group_ref, coeff_ref, local_ref, stage_ref, sect_ref,
+    held_ref, field_ref, dens_ref, going_ref, back_ref, recip_ref, moment_ref, row_ref, rows_ref,
+    tile_ref, gvec_tiles, band_tiles, dom_tiles, pair_ref, pairs_ref, square_ref, squares_ref,
     xg_ref, xh_ref, yg_ref, y_ref, depth_ref, zg_ref, zh_ref, scale_ref, place_ref, proj_ref,
     load_sem, local_sem, small_sem, own_sem, fsend, frecv, bsend, brecv, csend, crecv,
 ):
@@ -60,7 +61,7 @@
     total = band_size * gvec_size * dom_size
     x_local, extent, y_share, cap, live_total, atoms = plan
     band_id, gvec_id, dom_id = lax.axis_index("band"), lax.axis_index("gvec"), lax.axis_index("dom")
-    me = (band_id * gvec_size + gvec_id) * dom_size + dom_id
+    me = (dom_id * band_size + band_id) * gvec_size + gvec_id
     band_total = band_size * dom_size
     width = len(kernel_weights) * live_total
     cells = float(extent**3)
@@ -98,30 +99,33 @@
     gvec_at = [lax.rem(gvec_id + shift, gvec_size) for shift in range(gvec_size)]
     dom_at = [lax.rem(dom_id + shift, dom_size) for shift in range(dom_size)]
 
-    def peer_of(step):
-        outer = step // gvec_size
-        return band_at[outer // dom_size], gvec_at[step % gvec_size], dom_at[outer % dom_size]
-
-    for step in range(1, total):
-        pl.semaphore_signal(barrier, inc=1, device_id=peer_of(step), device_id_type=MESH)
-
-    def broadcast(kind, src, dst):
-        def copy_of(step):
-            return pltpu.make_async_remote_copy(
-                src_ref=src, dst_ref=dst.at[me],
-                send_sem=csend.at[kind, step], recv_sem=crecv.at[kind, step],
-                device_id=peer_of(step), device_id_type=MESH,
+    axis_peers = (
+        [(band_id, gvec_at[step], dom_id) for step in range(gvec_size)],
+        [(band_at[step], gvec_id, dom_id) for step in range(band_size)],
+        [(band_id, gvec_id, dom_at[step]) for step in range(dom_size)],
+    )
+    for peers in axis_peers:
+        for peer in peers[1:]:
+            pl.semaphore_signal(barrier, inc=1, device_id=peer, device_id_type=MESH)
+
+    def exchange(kind, axis, src, dst):
+        return [
+            pltpu.make_async_remote_copy(
+                src_ref=src, dst_ref=dst,
+                send_sem=csend.at[kind, axis, step], recv_sem=crecv.at[kind, axis, step],
+                device_id=axis_peers[axis][step], device_id_type=MESH,
             )
-
-        def start():
-            for step in range(1, total):
-                copy_of(step).start()
-
-        def wait(first, stop):
-            for step in range(first, stop):
-                copy_of(step).wait()
-
-        return start, wait
+            for step in range(1, len(axis_peers[axis]))
+        ]
+
+    def start_all(copies):
+        for copy in copies:
+            copy.start()
+        return copies
+
+    def wait_all(copies):
+        for copy in copies:
+            copy.wait()
 
     group = piece
     smalls[3].wait()
@@ -173,7 +177,7 @@
 
     if ahead:
         forward(0, 0)
-    pl.semaphore_wait(barrier, total - 1)
+    pl.semaphore_wait(barrier, band_size + gvec_size + dom_size - 3)
     if ahead:
         for step in range(1, gvec_size):
             lead_copy(step, 0).start()
@@ -199,9 +203,8 @@
     row = jnp.where(part, picked_charge, row)
     row = jnp.where(lane == 4 * cap, live.astype(F32), row)
     row_ref[...] = row
-    rows_ref[me] = row
-    start_rows, wait_rows = broadcast(0, row_ref, rows_ref)
-    start_rows()
+    rows_ref[dom_id, band_id, gvec_id] = row
+    copies = start_all(exchange(0, 0, row_ref, rows_ref.at[dom_id, band_id, gvec_id]))
 
     def lead(part, carry):
         forward(part, carry)
@@ -210,6 +213,8 @@
         return carry
 
     lax.fori_loop(1, ahead, lead, 0)
+    wait_all(copies)
+    copies = start_all(exchange(0, 1, rows_ref.at[dom_id, band_id], rows_ref.at[dom_id, band_id]))
     lax.fori_loop(ahead, pieces, forward, 0)
     for chunk in range(chunks):
         for step in range(1, gvec_size):
@@ -218,6 +223,8 @@
         sect_ref.at[pl.ds(gvec_id * y_share, y_share)], held_ref.at[gvec_id], own_sem.at[0]
     )
     own_copy.start()
+    wait_all(copies)
+    copies = start_all(exchange(0, 2, rows_ref.at[dom_id], rows_ref.at[dom_id]))
 
     local_copy.wait()
     x_block = 16
@@ -239,8 +246,8 @@
 
     lax.fori_loop(0, extent // x_block, turn_local, 0)
 
-    wait_rows(1, total)
-    rows = rows_ref[:, 0, :]
+    wait_all(copies)
+    rows = rows_ref[...].reshape(total, row_ref.shape[1])
     count = rows[:, 4 * cap : 4 * cap + 1]
     count_wide = jnp.broadcast_to(count, (total, live_total))
     offset = jnp.dot(group_ref[...], count_wide, precision=HIGH, preferred_element_type=F32)
@@ -315,6 +322,14 @@
             device_id=gvec_peer(step), device_id_type=MESH,
         )
 
+    def early_copy(step, chunk):
+        return pltpu.make_async_remote_copy(
+            src_ref=going_ref.at[chunk, pl.ds(gvec_at[step] * x_local, x_local)],
+            dst_ref=back_ref.at[gvec_id, chunk],
+            send_sem=bsend.at[step, chunk, 0], recv_sem=brecv.at[step, chunk, 0],
+            device_id=gvec_peer(step), device_id_type=MESH,
+        )
+
     def own_back(chunk):
         return pltpu.make_async_copy(
             going_ref.at[chunk, pl.ds(gvec_id * x_local, x_local)],
@@ -327,7 +342,7 @@
         for part in range(ahead):
             lead_copy(step, part).wait_recv()
 
-    def middle(chunk, carry):
+    def middle(chunk, inner):
         for step in range(1, gvec_size):
             forward_copy(step, chunk).wait_recv()
         for pair in range(y_chunk // 2):
@@ -344,29 +359,30 @@
             dens_ref[first] = square[:, :extent]
             dens_ref[first + 1] = square[:, extent:]
             fields = jnp.concatenate([field_ref[first], field_ref[first + 1]], axis=1)
-            result = dot(cos_ref[1], (fields * wide).astype(BF16))
+            applied = (fields * wide).astype(BF16)
+            result = dot(cos_ref[1], applied)
             stage_ref[pl.ds(2 * pair * extent, extent)] = result[:, :extent]
             stage_ref[pl.ds((2 * pair + 1) * extent, extent)] = result[:, extent:]
+            inner = inner + jnp.sum((applied.astype(F32) * wide).reshape(-1, 8, 2 * extent), axis=0)
 
         def spread(outer, inner_carry):
-            for inner in range(8):
-                a = outer * 8 + inner
+            for side in range(8):
+                a = outer * 8 + side
                 going_ref[chunk, a] = stage_ref[pl.ds(a, y_chunk, stride=extent)].astype(BF16)
             return inner_carry
 
         lax.fori_loop(0, extent // 8, spread, 0)
         own_back(chunk).start()
-        return carry
-
-    def middle_early(chunk, carry):
-        middle(chunk, carry)
-        for part in range(grains):
-            for step in range(1, gvec_size):
-                back_copy(step, chunk, part).start()
-        return carry
-
-    lax.fori_loop(0, early, middle_early, 0)
-    lax.fori_loop(early, chunks, middle, 0)
+        return inner
+
+    def middle_early(chunk, inner):
+        inner = middle(chunk, inner)
+        for step in range(1, gvec_size):
+            early_copy(step, chunk).start()
+        return inner
+
+    inner = lax.fori_loop(0, early, middle_early, jnp.zeros((8, 2 * extent), F32))
+    inner = lax.fori_loop(early, chunks, middle, inner)
 
     def send_late(part, carry):
         for chunk in range(early, chunks):
@@ -411,7 +427,14 @@
         moment_ref[1] * l_wave,
         moment_ref[0] * q_wave * l_wave,
     )
-    stress = [weight * total_of(term) / cells for term in terms]
+    terms = [total_of(term) for term in terms]
+    stress = [weight * term / cells for term in terms]
+    norm = total_of(moment_ref[0])
+    inner = total_of(inner) + 0.5 * (terms[0] + terms[1] + terms[2])
+    pair_ref[0:1] = jnp.broadcast_to(norm, (1, 128))
+    pair_ref[1:2] = jnp.broadcast_to(inner, (1, 128))
+    pairs_ref[gvec_id] = pair_ref[...]
+    pair_copies = start_all(exchange(2, 0, pair_ref, pairs_ref.at[gvec_id]))
 
     x_part = 32
 
@@ -450,52 +473,39 @@
     embedding = weight * jnp.sum(folded[3:4], axis=1, keepdims=True) / cells
     line = jnp.zeros((1, live_total), F32)
     tile_lane = iota((1, live_total), 1)
-    for at, value in enumerate(stress + [embedding]):
+    wait_all(pair_copies)
+    both = sum(pairs_ref[source] for source in range(gvec_size))
+    norm, inner = both[0:1], both[1:2]
+    energy = inner / norm
+    misc_ref[0:1] = energy
+    band_energy = weight * energy[:, 0:1] / float(gvec_size * band_total)
+    for at, value in enumerate(stress + [embedding, band_energy]):
         line = jnp.where(tile_lane == at, value, line)
     tile_ref[3:4] = line
-    tiles_ref[me] = tile_ref[...]
-    start_tiles, wait_tiles = broadcast(1, tile_ref, tiles_ref)
-    start_tiles()
+
+    def tile_stage(axis, slots, at):
+        slots[at] = tile_ref[...]
+        return start_all(exchange(1, axis, tile_ref, slots.at[at]))
+
+    def tile_sum(copies, slots):
+        wait_all(copies)
+        value = slots[0]
+        for source in range(1, slots.shape[0]):
+            value = value + slots[source]
+        tile_ref[...] = value
+
+    copies = tile_stage(0, gvec_tiles, gvec_id)
 
     for chunk in range(chunks):
         own_back(chunk).wait()
-    def force_to_atoms():
-        wait_tiles(1, total)
-        summed = tiles_ref[0]
-        for source in range(1, total):
-            summed = summed + tiles_ref[source]
-        slot_lanes = (iota((live_total, 128), 0).astype(F32) - place_ref[0:1, 0:1]) == iota(
-            (live_total, 128), 1
-        ).astype(F32)
-        slot_lanes = slot_lanes & (iota((live_total, 128), 1) < live)
-        slot_force = jnp.dot(summed, slot_lanes.astype(F32), precision=HIGH, preferred_element_type=F32)
-        near_column = jnp.full((128, 1), -1, jnp.int32)
-        for slot in range(cap):
-            near_column = jnp.where(iota((128, 1), 0) == slot, near_ref[slot], near_column)
-        at_atom = (iota((128, atoms), 1) == near_column).astype(F32)
-        atom_force = jnp.dot(slot_force, at_atom, precision=HIGH, preferred_element_type=F32)
-        force_out[...] = atom_force[0:3]
-        return summed
-
-    def merged(parts):
-        norm = sum(part[0] for part in parts)
-        inner = sum(part[1] for part in parts)
-        filled = norm > 0.0
-        energy = jnp.where(filled, inner / jnp.where(filled, norm, 1.0), 0.0)
-        square = 0.0
-        for part_norm, part_inner, part_square in parts:
-            filled = part_norm > 0.0
-            part_energy = jnp.where(filled, part_inner / jnp.where(filled, part_norm, 1.0), 0.0)
-            away = part_energy - energy
-            square = square + part_square + away * away * part_norm
-        return norm, inner, square
-
-    def image_of(part, sums):
-        for chunk in range(chunks):
+    for chunk in range(early):
+        for step in range(1, gvec_size):
+            early_copy(step, chunk).wait_recv()
+
+    def image_of(part, square):
+        for chunk in range(early, chunks):
             for step in range(1, gvec_size):
                 back_copy(step, chunk, part).wait_recv()
-        norm = jnp.zeros((8, extent), F32)
-        inner = jnp.zeros((8, extent), F32)
         for pair in range(grain // 2):
             first = part * grain + 2 * pair
             both = jnp.concatenate(
@@ -520,93 +530,83 @@
                 x_wave = x_wave_of(a)
                 image = (0.5 * x_wave * x_wave + plane_kinetic) * wide
                 image = image + waves[:, side * extent : (side + 1) * extent]
-                image_ref[a] = image
-                norm = norm + jnp.sum((wide * wide).reshape(-1, 8, extent), axis=0)
-                inner = inner + jnp.sum((wide * image).reshape(-1, 8, extent), axis=0)
-        norm, inner = total_of(norm), total_of(inner)
-        filled = norm > 0.0
-        energy = jnp.where(filled, inner / jnp.where(filled, norm, 1.0), 0.0)
-        square = jnp.zeros((8, extent), F32)
-        for side in range(grain):
-            a = part * grain + side
-            wide = coeff_ref[a].astype(F32)
-            image = image_ref[a]
-            residual = image - energy * wide
-            square = square + jnp.sum((residual * residual).reshape(-1, 8, extent), axis=0)
-            image_ref[a] = wide - image * recip_ref[a]
-        return merged([sums, (norm, inner, total_of(square))])
-
-    nothing = jnp.zeros((1, 1), F32)
-    sums = lax.fori_loop(0, grains - 1, image_of, (nothing, nothing, nothing))
-    summed = force_to_atoms()
-    own = image_of(grains - 1, sums)
-    for at, value in enumerate(own):
-        last_ref[at : at + 1] = jnp.broadcast_to(value, (1, 128))
-    lasts_ref[me] = last_ref[...]
-    start_last, wait_last = broadcast(2, last_ref, lasts_ref)
-    start_last()
-    wait_last(1, gvec_size)
-    parts = []
-    for source in range(gvec_size):
-        other = lasts_ref[(band_id * gvec_size + source) * dom_size + dom_id]
-        parts.append(tuple(other[at : at + 1] for at in range(3)))
-    norm, inner, square = merged(parts)
-    energy = inner / norm
-
-    def update(index, carry):
-        for side in range(4):
-            a = index * 4 + side
-            wide = coeff_ref[a].astype(F32)
-            waves_ref[0, a] = (image_ref[a] + energy * (wide * recip_ref[a])).astype(BF16)
-        return carry
-
-    lax.fori_loop(0, x_local // 4, update, 0)
-
-    wait_last(gvec_size, total)
-    band_sum = jnp.zeros((1, 128), F32)
-    for band in range(band_size):
-        for dom in range(dom_size):
-            both = 0.0
-            for source in range(gvec_size):
-                both = both + lasts_ref[(band * gvec_size + source) * dom_size + dom]
-            shifted = band * dom_size + dom - 0.5 * band_total
-            occupied = float(2.0 / (1.0 + np.exp(shifted / (0.125 * band_total))))
-            band_sum = band_sum + occupied * (both[1:2] / both[0:1])
-    misc_lane = iota((1, 128), 1)
-    misc_ref[0:1] = jnp.broadcast_to(energy, (1, 128))
-    misc_ref[1:2] = jnp.broadcast_to(square / norm, (1, 128))
-    misc_ref[2:3] = jnp.where(misc_lane == 7, band_sum / float(band_total), summed[3:4, :128])
+                residual = image - energy * wide
+                square = square + jnp.sum((residual * residual).reshape(-1, 8, extent), axis=0)
+                waves_ref[0, a] = (wide - residual * recip_ref[a]).astype(BF16)
+        return square
+
+    cuts = [(grains - 1) * at // 3 for at in range(4)]
+    square = lax.fori_loop(cuts[0], cuts[1], image_of, jnp.zeros((8, extent), F32))
+    tile_sum(copies, gvec_tiles)
+    copies = tile_stage(1, band_tiles, band_id)
+    square = lax.fori_loop(cuts[1], cuts[2], image_of, square)
+    tile_sum(copies, band_tiles)
+    copies = tile_stage(2, dom_tiles, dom_id)
+    square = lax.fori_loop(cuts[2], cuts[3], image_of, square)
+    tile_sum(copies, dom_tiles)
+
+    summed = tile_ref[...]
+    slot_lanes = (iota((live_total, 128), 0).astype(F32) - place_ref[0:1, 0:1]) == iota(
+        (live_total, 128), 1
+    ).astype(F32)
+    slot_lanes = slot_lanes & (iota((live_total, 128), 1) < live)
+    slot_force = jnp.dot(summed, slot_lanes.astype(F32), precision=HIGH, preferred_element_type=F32)
+    near_column = jnp.full((128, 1), -1, jnp.int32)
+    for slot in range(cap):
+        near_column = jnp.where(iota((128, 1), 0) == slot, near_ref[slot], near_column)
+    at_atom = (iota((128, atoms), 1) == near_column).astype(F32)
+    atom_force = jnp.dot(slot_force, at_atom, precision=HIGH, preferred_element_type=F32)
+    force_out[...] = atom_force[0:3]
+    misc_ref[2:3] = summed[3:4, 0:128]
     misc_ref[3:8] = jnp.zeros((5, 128), F32)
+
+    square = image_of(grains - 1, square)
+    square_ref[...] = jnp.broadcast_to(total_of(square), (1, 128))
+    squares_ref[gvec_id] = square_ref[...]
+    wait_all(start_all(exchange(3, 0, square_ref, squares_ref.at[gvec_id])))
+    square = sum(squares_ref[source] for source in range(gvec_size))
+    misc_ref[1:2] = square / norm
 
     for step in range(1, gvec_size):
         for part in range(ahead):
             lead_copy(step, part).wait_send()
         for chunk in range(chunks):
             forward_copy(step, chunk).wait_send()
+        for chunk in range(early):
+            early_copy(step, chunk).wait_send()
+        for chunk in range(early, chunks):
             for part in range(grains):
                 back_copy(step, chunk, part).wait_send()
 
 
-def finish_kernel(parts, waves_ref, force_ref, misc_ref, waves_hbm, energy_ref, ratio_ref, force_out, total_ref, sems):
+def finish_kernel(
+    parts, waves_ref, force_ref, misc_ref,
+    waves_hbm, force_hbm, energy_hbm, ratio_hbm, total_hbm, energy_ref, ratio_ref, total_ref, sems,
+):
     size = waves_ref.shape[1] // parts
-    copies = [
-        pltpu.make_async_copy(
-            waves_ref.at[:, pl.ds(part * size, size)], waves_hbm.at[:, pl.ds(part * size, size)], sems.at[part]
-        )
+    pairs = [
+        (waves_ref.at[:, pl.ds(part * size, size)], waves_hbm.at[:, pl.ds(part * size, size)])
         for part in range(parts)
     ]
-    for copy in copies:
+    pairs += [
+        (force_ref, force_hbm), (energy_ref, energy_hbm), (ratio_ref, ratio_hbm), (total_ref, total_hbm)
+    ]
+    copies = [
+        pltpu.make_async_copy(source, target, sems.at[at]) for at, (source, target) in enumerate(pairs)
+    ]
+    for copy in copies[: parts + 1]:
         copy.start()
     energy_ref[...] = misc_ref[0:1, 0:1]
     ratio_ref[...] = misc_ref[1:2, 0:1]
     total_ref[...] = misc_ref[2:3, 0:8]
-    force_out[...] = force_ref[...]
+    for copy in copies[parts + 1 :]:
+        copy.start()
     for copy in copies:
         copy.wait()
 
 
 def per_device(sizes, coeffs, v_local, atom_pos, atom_charge, near_list, live_count):
-    gvec_size = sizes[1]
+    band_size, gvec_size, dom_size = sizes
     total = sizes[0] * sizes[1] * sizes[2]
     local_bands, x_local, extent, _ = coeffs.shape
     assert local_bands == 1
@@ -636,15 +636,16 @@
             jnp.asarray(diagonal), jnp.asarray(groups), coeffs, v_local,
         )
     ]
-    waves_new, atom_force, misc = pl.pallas_call(
+    scalar = jax.ShapeDtypeStruct((1, 1), F32)
+    outs = (
+        jax.ShapeDtypeStruct(coeffs.shape, BF16), jax.ShapeDtypeStruct((3, atoms), F32),
+        scalar, scalar, jax.ShapeDtypeStruct((1, 8), F32),
+    )
+    results = pl.pallas_call(
         functools.partial(step_kernel, sizes, plan),
-        out_shape=(
-            jax.ShapeDtypeStruct(coeffs.shape, BF16),
-            jax.ShapeDtypeStruct((3, atoms), F32),
-            jax.ShapeDtypeStruct((8, 128), F32),
-        ),
+        out_shape=(outs[0], outs[1], jax.ShapeDtypeStruct((8, 128), F32)),
         in_specs=[hbm, smem] + [hbm] * 7,
-        out_specs=(vmem, vmem, vmem),
+        out_specs=(vmem,) * 3,
         scratch_shapes=[
             pltpu.SMEM(near_list.shape, jnp.int32),
             pltpu.VMEM(atom_pos.shape, F32),
@@ -662,14 +663,17 @@
             pltpu.VMEM((chunks, extent, y_chunk, extent), BF16),
             pltpu.VMEM((gvec_size, chunks, x_local, y_chunk, extent), BF16),
             pltpu.VMEM((x_local, extent, extent), F32),
-            pltpu.VMEM((x_local, extent, extent), F32),
             pltpu.VMEM((3, extent, extent), F32),
             pltpu.VMEM((1, lanes), F32),
-            pltpu.VMEM((total, 1, lanes), F32),
+            pltpu.VMEM((dom_size, band_size, gvec_size, 1, lanes), F32),
             pltpu.VMEM((4, live_total), F32),
-            pltpu.VMEM((total, 4, live_total), F32),
-            pltpu.VMEM((3, 128), F32),
-            pltpu.VMEM((total, 3, 128), F32),
+            pltpu.VMEM((gvec_size, 4, live_total), F32),
+            pltpu.VMEM((band_size, 4, live_total), F32),
+            pltpu.VMEM((dom_size, 4, live_total), F32),
+            pltpu.VMEM((2, 128), F32),
+            pltpu.VMEM((gvec_size, 2, 128), F32),
+            pltpu.VMEM((1, 128), F32),
+            pltpu.VMEM((gvec_size, 1, 128), F32),
             pltpu.VMEM((extent, width), F32),
             pltpu.VMEM((extent, width), F32),
             pltpu.VMEM((y_share, width), F32),
@@ -688,8 +692,8 @@
             dma((gvec_size, chunks + pieces // 2)),
             dma((gvec_size, chunks, grains)),
             dma((gvec_size, chunks, grains)),
-            dma((3, total)),
-            dma((3, total)),
+            dma((4, 3, max(sizes))),
+            dma((4, 3, max(sizes))),
         ],
         compiler_params=pltpu.CompilerParams(
             collective_id=0, has_side_effects=True, vmem_limit_bytes=36 * 1024 * 1024
@@ -697,19 +701,17 @@
         name="step",
     )(operands[0], live_count, *operands[1:])
     parts = 4 if x_local % 4 == 0 else 1
-    scalar = jax.ShapeDtypeStruct((1, 1), F32)
-    waves_new, energy, ratio, atom_force, totals = pl.pallas_call(
+    waves_new, atom_force, energy, ratio, totals = pl.pallas_call(
         functools.partial(finish_kernel, parts),
-        out_shape=(
-            jax.ShapeDtypeStruct(coeffs.shape, BF16), scalar, scalar,
-            jax.ShapeDtypeStruct((3, atoms), F32), jax.ShapeDtypeStruct((1, 8), F32),
-        ),
+        out_shape=outs,
         in_specs=[vmem] * 3,
-        out_specs=(hbm, vmem, vmem, vmem, vmem),
-        scratch_shapes=[dma((parts,))],
+        out_specs=(hbm,) * 5,
+        scratch_shapes=[
+            pltpu.VMEM((1, 1), F32), pltpu.VMEM((1, 1), F32), pltpu.VMEM((1, 8), F32), dma((parts + 4,)),
+        ],
         compiler_params=pltpu.CompilerParams(vmem_limit_bytes=8 * 1024 * 1024),
         name="finish",
-    )(waves_new, atom_force, misc)
+    )(*results)
     return (waves_new, energy.reshape(1), ratio.reshape(1), atom_force, totals.reshape(8))
 
 

time: 66.5 us -> 71.1 us (1.069)
  Pallas kernels: 65.1 us -> 69.7 us
    pallas_call x2, Pallas kernels: 65.1 us -> 69.7 us  [the longest x1 68.3 us: per_device(): pl.pallas_call(functools.partial(step_kernel, sizes, plan), out_shape=(ou...]
where the time goes in v4:
time: 71.1 us; the launch traced here: 71 us
  Pallas kernels  69.7 us (98%)
  between operations  1.29 us (2%)
    pallas_call x1, Pallas kernels, per_device(): pl.pallas_call(functools.partial(step_kernel, sizes, plan), out_shape=(ou...  68.3 us

profile of v4, /device:TPU:0, one launch (start us, length us, event | category | flops | bytes accessed | tf_op | source)
XLA Modules:
  0.0 71.0 jit_solution(10650886265493579029)
XLA Ops:
  1.3 68.3 %step.1 = (bf16[1,64,128,128]{3,2,1,0:T(8,128)(2,1)S(1)}, f32[3,1024]{1,0:T(4,128)S(1)}, f32[8,128]{1,0:T(8,128)S(1)}) custom-call(s32[16]{0:T(128)} %near_hbm.1, s32[1]{0:T(128)S(6)} %copy.14.live_ref, f32[3,1024]{1,0:T(4,128)} %pos_hbm.1, f32[1,1024]{1,0:T(1,128)} %bitcast.4, bf16[2,128,128]{2,1,0:T(8,128)(2,1)} %constant.6.clone.cos_hbm, ...), custom_call_target="tpu_custom_call" | custom-call | tf_op jit(solution)/shard_map/step/pallas_call | solution.py:644
  69.6 1.4 %finish.1 = (bf16[1,64,128,128]{3,2,1,0:T(8,128)(2,1)}, f32[3,1024]{1,0:T(4,128)}, f32[1,1]{1,0:T(1,128)}, f32[1,1]{1,0:T(1,128)}, f32[1,8]{1,0:T(1,128)}) custom-call(bf16[1,64,128,128]{3,2,1,0:T(8,128)(2,1)S(1)} %get-tuple-element.13.waves_ref, f32[3,1024]{1,0:T(4,128)S(1)} %get-tuple-element.14.force_ref, f32[8,128]{1,0:T(8,128)S(1)} %get-tuple-element.15.misc_ref), custom_call_target="tpu_custom_call" | custom-call | tf_op jit(solution)/shard_map/finish/pallas_call | solution.py:704

commit v5 on v4

--- a/solution.py
+++ b/solution.py
@@ -72,7 +72,7 @@
     pieces = x_local // piece
     grain = 8 if x_local % 8 == 0 else x_local
     grains = x_local // grain
-    early = max(chunks - 2, 0)
+    first_chunks, early = max(chunks - 3, 0), max(chunks - 2, 0)
     barrier = pltpu.get_barrier_semaphore()
 
     def load_of(part):
@@ -177,10 +177,6 @@
 
     if ahead:
         forward(0, 0)
-    pl.semaphore_wait(barrier, band_size + gvec_size + dom_size - 3)
-    if ahead:
-        for step in range(1, gvec_size):
-            lead_copy(step, 0).start()
 
     for at in (0, 1, 2, 5):
         smalls[at].wait()
@@ -192,19 +188,28 @@
         for slot in range(cap):
             near_row = jnp.where(lane == quantity * cap + slot, near_ref[slot], near_row)
     live = live_ref[0]
-    chosen = (iota((atoms, lanes), 0) == near_row).astype(F32)
-    picked_pos = jnp.dot(pos_ref[...], chosen, precision=HIGH, preferred_element_type=F32)
-    picked_charge = jnp.dot(charge_ref[...], chosen, precision=HIGH, preferred_element_type=F32)
+    chosen = (iota((atoms, lanes), 0) == near_row).astype(F32).astype(BF16)
+    values = jnp.concatenate([pos_ref[...], charge_ref[...]], axis=0)
+    high = values.astype(BF16)
+    rest = values - high.astype(F32)
+    middle_part = rest.astype(BF16)
+    low = (rest - middle_part.astype(F32)).astype(BF16)
+    picked = dot(high, chosen) + dot(middle_part, chosen) + dot(low, chosen)
     row = jnp.zeros((1, lanes), F32)
     for quantity in range(3):
         part = (lane >= quantity * cap) & (lane < (quantity + 1) * cap)
-        row = jnp.where(part, picked_pos[quantity : quantity + 1], row)
+        row = jnp.where(part, picked[quantity : quantity + 1], row)
     part = (lane >= 3 * cap) & (lane < 3 * cap + live) & (lane < 4 * cap)
-    row = jnp.where(part, picked_charge, row)
+    row = jnp.where(part, picked[3:4], row)
     row = jnp.where(lane == 4 * cap, live.astype(F32), row)
     row_ref[...] = row
     rows_ref[dom_id, band_id, gvec_id] = row
+
+    pl.semaphore_wait(barrier, band_size + gvec_size + dom_size - 3)
     copies = start_all(exchange(0, 0, row_ref, rows_ref.at[dom_id, band_id, gvec_id]))
+    if ahead:
+        for step in range(1, gvec_size):
+            lead_copy(step, 0).start()
 
     def lead(part, carry):
         forward(part, carry)
@@ -338,6 +343,45 @@
 
     own_copy.wait()
 
+    q_wave = iota((extent, extent), 0).astype(F32) * wave_step
+    l_wave = iota((extent, extent), 1).astype(F32) * wave_step
+    plane_kinetic = 0.5 * (q_wave * q_wave + l_wave * l_wave)
+    moment_ref[...] = jnp.zeros_like(moment_ref)
+
+    def x_wave_of(a):
+        return jnp.full((1, 1), gvec_id * x_local + a, jnp.int32).astype(F32) * wave_step
+
+    def coefficients(index, carry):
+        zero, one, two = 0.0, 0.0, 0.0
+        for inner in range(4):
+            a = index * 4 + inner
+            wide = coeff_ref[a].astype(F32)
+            x_wave = x_wave_of(a)
+            square = wide * wide
+            by_x = square * x_wave
+            zero, one, two = zero + square, one + by_x, two + by_x * x_wave
+            recip_ref[a] = step_size / (1.0 + 0.5 * x_wave * x_wave + plane_kinetic)
+        moment_ref[0] += zero
+        moment_ref[1] += one
+        moment_ref[2] += two
+        return carry
+
+    lax.fori_loop(0, x_local // 4, coefficients, 0)
+    group_id = band_id * dom_size + dom_id
+    shifted = jnp.full((1, 1), group_id, jnp.int32).astype(F32) - 0.5 * band_total
+    weight = 2.0 / (1.0 + jnp.exp(shifted / (0.125 * band_total)))
+    terms = (
+        moment_ref[2],
+        moment_ref[0] * q_wave * q_wave,
+        moment_ref[0] * l_wave * l_wave,
+        moment_ref[1] * q_wave,
+        moment_ref[1] * l_wave,
+        moment_ref[0] * q_wave * l_wave,
+    )
+    terms = [total_of(term) for term in terms]
+    stress = [weight * term / cells for term in terms]
+    norm = total_of(moment_ref[0])
+
     for step in range(1, gvec_size):
         for part in range(ahead):
             lead_copy(step, part).wait_recv()
@@ -381,60 +425,17 @@
             early_copy(step, chunk).start()
         return inner
 
-    inner = lax.fori_loop(0, early, middle_early, jnp.zeros((8, 2 * extent), F32))
-    inner = lax.fori_loop(early, chunks, middle, inner)
-
-    def send_late(part, carry):
-        for chunk in range(early, chunks):
-            for step in range(1, gvec_size):
-                back_copy(step, chunk, part).start()
-        return carry
-
-    lax.fori_loop(0, grains, send_late, 0)
-
-    q_wave = iota((extent, extent), 0).astype(F32) * wave_step
-    l_wave = iota((extent, extent), 1).astype(F32) * wave_step
-    plane_kinetic = 0.5 * (q_wave * q_wave + l_wave * l_wave)
-    moment_ref[...] = jnp.zeros_like(moment_ref)
-
-    def x_wave_of(a):
-        return jnp.full((1, 1), gvec_id * x_local + a, jnp.int32).astype(F32) * wave_step
-
-    def coefficients(index, carry):
-        zero, one, two = 0.0, 0.0, 0.0
-        for inner in range(4):
-            a = index * 4 + inner
-            wide = coeff_ref[a].astype(F32)
-            x_wave = x_wave_of(a)
-            square = wide * wide
-            by_x = square * x_wave
-            zero, one, two = zero + square, one + by_x, two + by_x * x_wave
-            recip_ref[a] = step_size / (1.0 + 0.5 * x_wave * x_wave + plane_kinetic)
-        moment_ref[0] += zero
-        moment_ref[1] += one
-        moment_ref[2] += two
-        return carry
-
-    lax.fori_loop(0, x_local // 4, coefficients, 0)
-    group_id = band_id * dom_size + dom_id
-    shifted = jnp.full((1, 1), group_id, jnp.int32).astype(F32) - 0.5 * band_total
-    weight = 2.0 / (1.0 + jnp.exp(shifted / (0.125 * band_total)))
-    terms = (
-        moment_ref[2],
-        moment_ref[0] * q_wave * q_wave,
-        moment_ref[0] * l_wave * l_wave,
-        moment_ref[1] * q_wave,
-        moment_ref[1] * l_wave,
-        moment_ref[0] * q_wave * l_wave,
-    )
-    terms = [total_of(term) for term in terms]
-    stress = [weight * term / cells for term in terms]
-    norm = total_of(moment_ref[0])
+    inner = lax.fori_loop(0, first_chunks, middle_early, jnp.zeros((8, 2 * extent), F32))
+    inner = lax.fori_loop(first_chunks, chunks, middle, inner)
+
     inner = total_of(inner) + 0.5 * (terms[0] + terms[1] + terms[2])
     pair_ref[0:1] = jnp.broadcast_to(norm, (1, 128))
     pair_ref[1:2] = jnp.broadcast_to(inner, (1, 128))
     pairs_ref[gvec_id] = pair_ref[...]
     pair_copies = start_all(exchange(2, 0, pair_ref, pairs_ref.at[gvec_id]))
+    for chunk in range(first_chunks, early):
+        for step in range(1, gvec_size):
+            early_copy(step, chunk).start()
 
     x_part = 32
 
@@ -495,6 +496,14 @@
         tile_ref[...] = value
 
     copies = tile_stage(0, gvec_tiles, gvec_id)
+
+    def send_late(part, carry):
+        for chunk in range(early, chunks):
+            for step in range(1, gvec_size):
+                back_copy(step, chunk, part).start()
+        return carry
+
+    lax.fori_loop(0, grains, send_late, 0)
 
     for chunk in range(chunks):
         own_back(chunk).wait()

time: 71.1 us -> 62.8 us (0.88)
  Pallas kernels: 69.7 us -> 61.4 us
    pallas_call x1, Pallas kernels: 68.3 us -> 60 us  [per_device(): pl.pallas_call(functools.partial(step_kernel, sizes, plan), out_shape=(ou...]
where the time goes in v5:
time: 62.8 us; the launch traced here: 62.7 us
  Pallas kernels  61.4 us (98%)
  between operations  1.29 us (2%)
    pallas_call x1, Pallas kernels, per_device(): pl.pallas_call(functools.partial(step_kernel, sizes, plan), out_shape=(ou...  60 us
    pallas_call x1, Pallas kernels, per_device(): pl.pallas_call(functools.partial(finish_kernel, parts), out_shape=outs, i...  1.39 us

profile of v5, /device:TPU:0, one launch (start us, length us, event | category | flops | bytes accessed | tf_op | source)
XLA Modules:
  0.0 62.7 jit_solution(11441696279271274923)
XLA Ops:
  1.3 60.0 %step.1 = (bf16[1,64,128,128]{3,2,1,0:T(8,128)(2,1)S(1)}, f32[3,1024]{1,0:T(4,128)S(1)}, f32[8,128]{1,0:T(8,128)S(1)}) custom-call(s32[16]{0:T(128)} %near_hbm.1, s32[1]{0:T(128)S(6)} %copy.14.live_ref, f32[3,1024]{1,0:T(4,128)} %pos_hbm.1, f32[1,1024]{1,0:T(1,128)} %bitcast.4, bf16[2,128,128]{2,1,0:T(8,128)(2,1)} %constant.6.clone.cos_hbm, ...), custom_call_target="tpu_custom_call" | custom-call | tf_op jit(solution)/shard_map/step/pallas_call | solution.py:653
  61.3 1.4 %finish.1 = (bf16[1,64,128,128]{3,2,1,0:T(8,128)(2,1)}, f32[3,1024]{1,0:T(4,128)}, f32[1,1]{1,0:T(1,128)}, f32[1,1]{1,0:T(1,128)}, f32[1,8]{1,0:T(1,128)}) custom-call(bf16[1,64,128,128]{3,2,1,0:T(8,128)(2,1)S(1)} %get-tuple-element.13.waves_ref, f32[3,1024]{1,0:T(4,128)S(1)} %get-tuple-element.14.force_ref, f32[8,128]{1,0:T(8,128)S(1)} %get-tuple-element.15.misc_ref), custom_call_target="tpu_custom_call" | custom-call | tf_op jit(solution)/shard_map/finish/pallas_call | solution.py:713
